TPU v7x, 256 devices: a whole 4x4x8 slice. The times are simulated.
256 devices in a mesh: dp: 8 (over y, core), ctx: 32 (over x, z).
Axes of the slice: x: 4, y: 4, z: 8, core: 2. Of those that a mesh axis runs over, the one named last changes fastest.
Arguments:
- features: bfloat16 [8, 4096, 1536], P('dp', 'ctx'), may hold values from -6 to 6
- short_weight: float32 [7, 1536], replicated, may hold values from -2 to 2
- long_filter: float32 [4096, 512], P('ctx'), may hold values from -4 to 4
- skip_bias: float32 [512], replicated, may hold values from 0.5 to 1.5
- cotangent: bfloat16 [8, 4096, 512], P('dp', 'ctx'), may hold values from -6 to 6
Outputs:
- layer_out: bfloat16 [8, 4096, 512], P('dp', 'ctx')
- grad_features: bfloat16 [8, 4096, 1536], P('dp', 'ctx')
- grad_short: float32 [7, 1536], replicated
- grad_filter: float32 [4096, 512], P('ctx')
- grad_skip: float32 [512], replicated
All inputs are finite; a program needn't handle non-finite values.
Results may differ from a plain program's by a relative error of at most 0.001.
Values may be sent and summed in bfloat16 or wider, within the bound.
A program may use at most 64 MiB of HBM per device.

v0:
```python
import math

import jax
import jax.numpy as jnp
from jax import lax
from jax.sharding import PartitionSpec as P

PRECISE = lax.Precision.HIGHEST


def swapped(value, axis, distance):
    mask = 2**distance
    pairs = [(source, source ^ mask) for source in range(lax.axis_size(axis))]
    return lax.ppermute(value, axis, pairs)


def shifted(value, axis, steps):
    count = lax.axis_size(axis)
    initial, last = (max(0, -steps), min(count, count - steps))
    return lax.ppermute(value, axis, [(source, source + steps) for source in range(initial, last)])


def bit_reverse(index_value, bit_count):
    reversed_value = jnp.zeros_like(index_value)
    for bit_place in range(bit_count):
        digit_now = index_value // 2**bit_place % 2
        reversed_value = reversed_value + digit_now * 2 ** (bit_count - 1 - bit_place)
    return reversed_value


def spectral_table(device, parts_count, tokens):
    bit_count = parts_count.bit_length() - 1
    coarse_freq = 2 * bit_reverse(device, bit_count) + jnp.arange(2, dtype=jnp.int32)
    total_points = 2 * parts_count * tokens
    column_index = jnp.arange(tokens, dtype=jnp.int32)
    full_freq = coarse_freq[:, None] + 2 * parts_count * column_index[None, :]
    phase_value = column_index[None, None, :] * full_freq[:, :, None] % total_points
    angle_value = phase_value.astype(jnp.float32) * (2.0 * math.pi / total_points)
    return (jnp.cos(angle_value), -jnp.sin(angle_value))


def contract(matrix, values):
    return jnp.einsum("akm,amw->akw", matrix, values, precision=PRECISE)


def contract_back(matrix, values):
    return jnp.einsum("akm,akw->amw", matrix, values, precision=PRECISE)


def local_forward(spec_real, spec_imag, table):
    table_real, table_imag = table
    out_real = contract(table_real, spec_real) - contract(table_imag, spec_imag)
    out_imag = contract(table_real, spec_imag) + contract(table_imag, spec_real)
    return (out_real, out_imag)


def local_inverse(spec_real, spec_imag, table):
    table_real, table_imag = table
    factor = 1.0 / spec_real.shape[1]
    out_real = (
        contract_back(table_real, spec_real) + contract_back(table_imag, spec_imag)
    ) * factor
    out_imag = (
        contract_back(table_real, spec_imag) - contract_back(table_imag, spec_real)
    ) * factor
    return (out_real, out_imag)


def pair_swap(stacked, bit_place):
    return swapped(stacked, "ctx", bit_place)


def pair_swap_back(stacked, bit_place):
    return swapped(stacked, "ctx", bit_place)


def section_terms(device, bit_place):
    span_size = 2**bit_place
    upper_flag = device // span_size % 2
    sign_value = (1 - 2 * upper_flag).astype(jnp.float32)
    turn_value = math.pi / span_size * (upper_flag * (device % span_size)).astype(jnp.float32)
    return (sign_value, jnp.cos(turn_value), jnp.sin(turn_value))


def butterfly_forward(signals):
    parts_count = lax.axis_size("ctx")
    device = lax.axis_index("ctx")
    bit_count = parts_count.bit_length() - 1
    angle_value = math.pi * device.astype(jnp.float32) / parts_count
    spec_real = jnp.stack([signals, signals * jnp.cos(angle_value)])
    spec_imag = jnp.stack([jnp.zeros_like(signals), -signals * jnp.sin(angle_value)])
    for bit_place in reversed(range(bit_count)):
        sign_value, cos_turn, sin_turn = section_terms(device, bit_place)
        partner = pair_swap(jnp.stack([spec_real, spec_imag]), bit_place)
        joined_real = partner[0] + sign_value * spec_real
        joined_imag = partner[1] + sign_value * spec_imag
        spec_real = joined_real * cos_turn + joined_imag * sin_turn
        spec_imag = joined_imag * cos_turn - joined_real * sin_turn
    return (spec_real, spec_imag)


def butterfly_inverse(spec_real, spec_imag):
    parts_count = lax.axis_size("ctx")
    device = lax.axis_index("ctx")
    bit_count = parts_count.bit_length() - 1
    for bit_place in range(bit_count):
        sign_value, cos_turn, sin_turn = section_terms(device, bit_place)
        turned_real = spec_real * cos_turn - spec_imag * sin_turn
        turned_imag = spec_imag * cos_turn + spec_real * sin_turn
        partner = pair_swap_back(jnp.stack([turned_real, turned_imag]), bit_place)
        spec_real = 0.5 * (partner[0] + sign_value * turned_real)
        spec_imag = 0.5 * (partner[1] + sign_value * turned_imag)
    angle_value = math.pi * device.astype(jnp.float32) / parts_count
    cos_last = jnp.cos(angle_value)
    sin_last = jnp.sin(angle_value)
    out_real = 0.5 * (spec_real[0] + spec_real[1] * cos_last - spec_imag[1] * sin_last)
    out_imag = 0.5 * (spec_imag[0] + spec_imag[1] * cos_last + spec_real[1] * sin_last)
    return (out_real, out_imag)


def per_device(features, short_weight, long_filter, skip_bias, cotangent):
    taps = short_weight.shape[0]
    token_rows = features[0]
    tokens = token_rows.shape[0]
    channels = long_filter.shape[1]
    parts_count = lax.axis_size("ctx")
    device = lax.axis_index("ctx")
    history = shifted(token_rows[tokens - (taps - 1) :], "ctx", 1)
    extended = jnp.concatenate([history, token_rows], axis=0).astype(jnp.float32)
    mixed_feats = jnp.zeros((tokens, token_rows.shape[1]), jnp.float32)
    for tap_index in range(taps):
        start_row = taps - 1 - tap_index
        mixed_feats = (
            mixed_feats + short_weight[tap_index] * extended[start_row : start_row + tokens]
        )
    query = mixed_feats[:, :channels]
    key_part = mixed_feats[:, channels : 2 * channels]
    value_part = mixed_feats[:, 2 * channels :]
    gated = key_part * value_part
    upstream = cotangent[0].astype(jnp.float32)
    dconv = upstream * query
    signals = jnp.concatenate([gated, long_filter, dconv], axis=1)
    table = spectral_table(device, parts_count, tokens)
    spec_real, spec_imag = butterfly_forward(signals)
    spec_real, spec_imag = local_forward(spec_real, spec_imag, table)
    gated_real = spec_real[..., :channels]
    gated_imag = spec_imag[..., :channels]
    filter_real = spec_real[..., channels : 2 * channels]
    filter_imag = spec_imag[..., channels : 2 * channels]
    dconv_real = spec_real[..., 2 * channels :]
    dconv_imag = spec_imag[..., 2 * channels :]
    conv_real = gated_real * filter_real - gated_imag * filter_imag
    conv_imag = gated_real * filter_imag + gated_imag * filter_real
    back_real = filter_real * dconv_real + filter_imag * dconv_imag
    back_imag = filter_real * dconv_imag - filter_imag * dconv_real
    corr_real = gated_real * dconv_real + gated_imag * dconv_imag
    corr_imag = gated_real * dconv_imag - gated_imag * dconv_real
    inverse_real = jnp.concatenate([conv_real - back_imag, corr_real], axis=-1)
    inverse_imag = jnp.concatenate([conv_imag + back_real, corr_imag], axis=-1)
    inverse_real, inverse_imag = local_inverse(inverse_real, inverse_imag, table)
    result_real, result_imag = butterfly_inverse(inverse_real, inverse_imag)
    long_conv = result_real[:, :channels] + skip_bias * gated
    dgated = result_imag[:, :channels] + skip_bias * dconv
    filter_part = result_real[:, channels:]
    layer_out = (query * long_conv).astype(jnp.bfloat16)[None]
    dmixed = jnp.concatenate([upstream * long_conv, dgated * value_part, dgated * key_part], axis=1)
    later = shifted(dmixed[: taps - 1], "ctx", -1)
    ahead = jnp.concatenate([dmixed, later], axis=0)
    grad_local = jnp.zeros_like(dmixed)
    short_rows = []
    for tap_index in range(taps):
        grad_local = grad_local + short_weight[tap_index] * ahead[tap_index : tap_index + tokens]
        start_row = taps - 1 - tap_index
        short_rows.append(jnp.sum(dmixed * extended[start_row : start_row + tokens], axis=0))
    grad_features = grad_local.astype(jnp.bfloat16)[None]
    short_part = jnp.stack(short_rows)
    skip_part = jnp.sum(dconv * gated, axis=0)
    scale = 1.0 / math.sqrt(lax.axis_size("dp") * parts_count * tokens)
    filter_sum = lax.psum(filter_part, "dp")
    short_sum, skip_sum = lax.psum((short_part, skip_part), ("dp", "ctx"))
    return (layer_out, grad_features, short_sum * scale, filter_sum * scale, skip_sum * scale)


def solution(mesh):
    return jax.shard_map(
        per_device,
        mesh=mesh,
        in_specs=(P("dp", "ctx", None), P(), P("ctx", None), P(), P("dp", "ctx", None)),
        out_specs=(P("dp", "ctx", None), P("dp", "ctx", None), P(), P("ctx", None), P()),
        check_vma=False,
    )
```

profile of v0, /device:TPU:1, one launch (start us, length us, event | category | flops | bytes accessed | tf_op | source)
XLA Modules:
  0.0 1048.7 jit_solution(7923902592177502704)
XLA Ops:
  8.0 4.4 collective-permute-start
  12.3 1.3 slice_reduce_fusion.6
  18.3 1.9 pad_maximum_fusion
  20.2 6.4 collective-permute-start.1
  26.8 67.0 %collective-permute-done.1 = f32[2,2,128,1536]{3,2,1,0:T(8,128)} collective-permute-done((f32[2,2,128,1536]{3,2,1,0:T(8,128)}, f32[2,2,128,1536]{3,2,1,0:T(8,128)}, u32[]{:S(2)}, u32[]{:S(2)}) %collective-permute-start.1) | collective-permute-done | bytes 3145760 | tf_op jit(solution)/shard_map/ppermute | solution.py:14
  93.8 3.0 multiply_subtract_fusion.4
  96.8 2.0 pad_maximum_fusion.1
  100.2 66.4 %collective-permute-done.2 = f32[2,2,128,1536]{3,2,1,0:T(8,128)} collective-permute-done((f32[2,2,128,1536]{3,2,1,0:T(8,128)}, f32[2,2,128,1536]{3,2,1,0:T(8,128)}, u32[]{:S(2)}, u32[]{:S(2)}) %collective-permute-start.2) | collective-permute-done | bytes 3145760 | tf_op jit(solution)/shard_map/ppermute | solution.py:14
  166.6 3.1 multiply_subtract_fusion.3
  169.7 2.1 pad_maximum_fusion.2
  172.4 3.1 collective-permute-start.3
  175.7 138.0 %collective-permute-done.3 = f32[2,2,128,1536]{3,2,1,0:T(8,128)} collective-permute-done((f32[2,2,128,1536]{3,2,1,0:T(8,128)}, f32[2,2,128,1536]{3,2,1,0:T(8,128)}, u32[]{:S(2)}, u32[]{:S(2)}) %collective-permute-start.3) | collective-permute-done | bytes 3145760 | tf_op jit(solution)/shard_map/ppermute | solution.py:14
  313.7 3.6 multiply_subtract_fusion.2
  317.4 2.1 pad_maximum_fusion.3
  319.7 138.1 %collective-permute-done.4 = f32[2,2,128,1536]{3,2,1,0:T(8,128)} collective-permute-done((f32[2,2,128,1536]{3,2,1,0:T(8,128)}, f32[2,2,128,1536]{3,2,1,0:T(8,128)}, u32[]{:S(2)}, u32[]{:S(2)}) %collective-permute-start.4) | collective-permute-done | bytes 3145760 | tf_op jit(solution)/shard_map/ppermute | solution.py:14
  457.7 3.1 multiply_add_fusion.1
  460.8 2.0 pad_maximum_fusion.4
  463.6 68.9 %collective-permute-done.5 = f32[2,2,128,1536]{3,2,1,0:T(8,128)} collective-permute-done((f32[2,2,128,1536]{3,2,1,0:T(8,128)}, f32[2,2,128,1536]{3,2,1,0:T(8,128)}, u32[]{:S(2)}, u32[]{:S(2)}) %collective-permute-start.5) | collective-permute-done | bytes 3145760 | tf_op jit(solution)/shard_map/ppermute | solution.py:14
  532.5 3.5 fusion.2
  536.0 2.0 fusion.32
  538.0 2.0 fusion.33
  540.0 2.0 convolution_add_fusion
  541.9 2.0 convolution_subtract_fusion
  544.6 1.5 fusion.24
  546.1 1.7 fusion.23
  547.8 1.5 convolution_add_fusion.1
  549.4 1.5 convolution_subtract_fusion.1
  551.1 1.5 pad_maximum_fusion.5
  552.9 45.3 %collective-permute-done.6 = f32[2,2,128,1024]{3,2,1,0:T(8,128)} collective-permute-done((f32[2,2,128,1024]{3,2,1,0:T(8,128)}, f32[2,2,128,1024]{3,2,1,0:T(8,128)}, u32[]{:S(2)}, u32[]{:S(2)}) %collective-permute-start.6) | collective-permute-done | bytes 2097184 | tf_op jit(solution)/shard_map/ppermute | solution.py:14
  598.2 2.0 multiply_add_fusion.8
  601.3 1.5 pad_maximum_fusion.6
  602.8 1.7 collective-permute-start.7
  604.5 91.5 %collective-permute-done.7 = f32[2,2,128,1024]{3,2,1,0:T(8,128)} collective-permute-done((f32[2,2,128,1024]{3,2,1,0:T(8,128)}, f32[2,2,128,1024]{3,2,1,0:T(8,128)}, u32[]{:S(2)}, u32[]{:S(2)}) %collective-permute-start.7) | collective-permute-done | bytes 2097184 | tf_op jit(solution)/shard_map/ppermute | solution.py:14
  696.1 2.3 multiply_add_fusion.7
  699.7 2.4 collective-permute-start.8
  702.1 93.4 %collective-permute-done.8 = f32[2,2,128,1024]{3,2,1,0:T(8,128)} collective-permute-done((f32[2,2,128,1024]{3,2,1,0:T(8,128)S(1)}, f32[2,2,128,1024]{3,2,1,0:T(8,128)}, u32[]{:S(2)}, u32[]{:S(2)}) %collective-permute-start.8) | collective-permute-done | bytes 2097184 | tf_op jit(solution)/shard_map/ppermute | solution.py:14
  795.5 2.7 multiply_add_fusion.6
  798.2 1.5 pad_maximum_fusion.8
  799.9 46.8 %collective-permute-done.9 = f32[2,2,128,1024]{3,2,1,0:T(8,128)} collective-permute-done((f32[2,2,128,1024]{3,2,1,0:T(8,128)}, f32[2,2,128,1024]{3,2,1,0:T(8,128)}, u32[]{:S(2)}, u32[]{:S(2)}) %collective-permute-start.9) | collective-permute-done | bytes 2097184 | tf_op jit(solution)/shard_map/ppermute | solution.py:14
  846.7 2.0 multiply_subtract_fusion.5
  849.0 2.1 collective-permute-start.10
  851.1 45.3 %collective-permute-done.10 = f32[2,2,128,1024]{3,2,1,0:T(8,128)S(1)} collective-permute-done((f32[2,2,128,1024]{3,2,1,0:T(8,128)S(1)}, f32[2,2,128,1024]{3,2,1,0:T(8,128)S(1)}, u32[]{:S(2)}, u32[]{:S(2)}) %collective-permute-start.10) | collective-permute-done | bytes 2097184 | tf_op jit(solution)/shard_map/ppermute | solution.py:14
  900.1 76.6 %all-reduce.1 = (f32[7,1536]{1,0:T(8,128)S(1)}, f32[512]{0:T(512)S(1)}) all-reduce(f32[7,1536]{1,0:T(8,128)S(1)} %stack.165, f32[512]{0:T(512)S(1)} %get-tuple-element.21), channel_id=1, replica_groups=mesh['dp'=8,'ctx'=32] {'dp','ctx'}, use_global_device_ids=true, to_apply=%region_7.8 | all-reduce | flops 11264 | bytes 90112 | tf_op jit(solution)/shard_map/psum | solution.py:180
  977.4 1.3 collective-permute-start.11
  979.3 3.3 collective-permute-done.11
  982.6 1.4 fusion.41
  984.0 56.2 %all-reduce.4.cloned.1.call-done = f32[128,512]{1,0:T(8,128)} async-done(((f32[128,512]{1,0:T(8,128)}), f32[128,512]{1,0:T(8,128)}) %all-reduce.4.cloned.1.call-update) | async-done | bytes 262160 | tf_op jit(solution)/shard_map/psum | solution.py:179
  1040.2 1.7 broadcast_multiply_fusion
  (78 shorter events, 16.7 us)
Async XLA Ops:
  7.2 1033.1 %all-reduce.4.cloned.1.call-start = ((), (), s32[]{:S(2)}) async-start(), calls=%async_computation | async-start | bytes 524288 | tf_op jit(solution)/shard_map/psum | solution.py:179
  8.0 5.8 collective-permute-start
  14.9 0.9 copy-start.16
  15.8 1.4 copy-start.9
  15.8 1.1 copy-start.15
  15.9 1.3 copy-start.13
  17.2 0.9 copy-start.11
  17.2 1.1 copy-start.12
  20.2 73.6 %collective-permute-start.1 = (f32[2,2,128,1536]{3,2,1,0:T(8,128)}, f32[2,2,128,1536]{3,2,1,0:T(8,128)}, u32[]{:S(2)}, u32[]{:S(2)}) collective-permute-start(f32[2,2,128,1536]{3,2,1,0:T(8,128)} %pad_maximum_fusion), channel_id=1, source_target_pairs={{0,16},{1,17},{2,18},{3,19},{4,20},{5,21},{6,22},{7,23},{8,24},{9,... | collective-permute-start | bytes 9437192 | tf_op jit(solution)/shard_map/ppermute | solution.py:14
  96.8 2.1 copy-start.1
  98.9 67.7 %collective-permute-start.2 = (f32[2,2,128,1536]{3,2,1,0:T(8,128)}, f32[2,2,128,1536]{3,2,1,0:T(8,128)}, u32[]{:S(2)}, u32[]{:S(2)}) collective-permute-start(f32[2,2,128,1536]{3,2,1,0:T(8,128)} %pad_maximum_fusion.1), channel_id=1, source_target_pairs={{0,8},{1,9},{2,10},{3,11},{4,12},{5,13},{6,14},{7,15},{8,0},{9,1},... | collective-permute-start | bytes 9437192 | tf_op jit(solution)/shard_map/ppermute | solution.py:14
  169.7 2.3 copy-start.2
  169.7 2.7 copy-start.3
  172.4 141.3 %collective-permute-start.3 = (f32[2,2,128,1536]{3,2,1,0:T(8,128)}, f32[2,2,128,1536]{3,2,1,0:T(8,128)}, u32[]{:S(2)}, u32[]{:S(2)}) collective-permute-start(f32[2,2,128,1536]{3,2,1,0:T(8,128)} %pad_maximum_fusion.2), channel_id=1, source_target_pairs={{0,4},{1,5},{2,6},{3,7},{4,0},{5,1},{6,2},{7,3},{8,12},{9,13},{10,... | collective-permute-start | bytes 9437192 | tf_op jit(solution)/shard_map/ppermute | solution.py:14
  317.4 2.1 copy-start
  319.5 138.2 %collective-permute-start.4 = (f32[2,2,128,1536]{3,2,1,0:T(8,128)}, f32[2,2,128,1536]{3,2,1,0:T(8,128)}, u32[]{:S(2)}, u32[]{:S(2)}) collective-permute-start(f32[2,2,128,1536]{3,2,1,0:T(8,128)} %pad_maximum_fusion.3), channel_id=1, source_target_pairs={{0,2},{1,3},{2,0},{3,1},{4,6},{5,7},{6,4},{7,5},{8,10},{9,11},{10,... | collective-permute-start | bytes 9437192 | tf_op jit(solution)/shard_map/ppermute | solution.py:14
  460.8 2.1 copy-start.4
  460.8 2.7 copy-start.5
  463.5 69.0 %collective-permute-start.5 = (f32[2,2,128,1536]{3,2,1,0:T(8,128)}, f32[2,2,128,1536]{3,2,1,0:T(8,128)}, u32[]{:S(2)}, u32[]{:S(2)}) collective-permute-start(f32[2,2,128,1536]{3,2,1,0:T(8,128)} %pad_maximum_fusion.4), channel_id=1, source_target_pairs={{0,1},{1,0},{2,3},{3,2},{4,5},{5,4},{6,7},{7,6},{8,9},{9,8},{10,11... | collective-permute-start | bytes 9437192 | tf_op jit(solution)/shard_map/ppermute | solution.py:14
  552.6 45.6 %collective-permute-start.6 = (f32[2,2,128,1024]{3,2,1,0:T(8,128)}, f32[2,2,128,1024]{3,2,1,0:T(8,128)}, u32[]{:S(2)}, u32[]{:S(2)}) collective-permute-start(f32[2,2,128,1024]{3,2,1,0:T(8,128)} %pad_maximum_fusion.5), channel_id=1, source_target_pairs={{0,1},{1,0},{2,3},{3,2},{4,5},{5,4},{6,7},{7,6},{8,9},{9,8},{10,11... | collective-permute-start | bytes 6291464 | tf_op jit(solution)/shard_map/ppermute | solution.py:14
  600.3 1.0 copy-start.6
  602.8 93.3 %collective-permute-start.7 = (f32[2,2,128,1024]{3,2,1,0:T(8,128)}, f32[2,2,128,1024]{3,2,1,0:T(8,128)}, u32[]{:S(2)}, u32[]{:S(2)}) collective-permute-start(f32[2,2,128,1024]{3,2,1,0:T(8,128)} %pad_maximum_fusion.6), channel_id=1, source_target_pairs={{0,2},{1,3},{2,0},{3,1},{4,6},{5,7},{6,4},{7,5},{8,10},{9,11},{10,... | collective-permute-start | bytes 6291464 | tf_op jit(solution)/shard_map/ppermute | solution.py:14
  698.4 1.0 copy-start.7
  698.4 1.3 copy-start.8
  699.7 95.8 %collective-permute-start.8 = (f32[2,2,128,1024]{3,2,1,0:T(8,128)S(1)}, f32[2,2,128,1024]{3,2,1,0:T(8,128)}, u32[]{:S(2)}, u32[]{:S(2)}) collective-permute-start(f32[2,2,128,1024]{3,2,1,0:T(8,128)S(1)} %pad_maximum_fusion.7), channel_id=1, source_target_pairs={{0,4},{1,5},{2,6},{3,7},{4,0},{5,1},{6,2},{7,3},{8,12},{9,13},{10,... | collective-permute-start | bytes 6291464 | tf_op jit(solution)/shard_map/ppermute | solution.py:14
  799.7 47.0 %collective-permute-start.9 = (f32[2,2,128,1024]{3,2,1,0:T(8,128)}, f32[2,2,128,1024]{3,2,1,0:T(8,128)}, u32[]{:S(2)}, u32[]{:S(2)}) collective-permute-start(f32[2,2,128,1024]{3,2,1,0:T(8,128)} %pad_maximum_fusion.8), channel_id=1, source_target_pairs={{0,8},{1,9},{2,10},{3,11},{4,12},{5,13},{6,14},{7,15},{8,0},{9,1},... | collective-permute-start | bytes 6291464 | tf_op jit(solution)/shard_map/ppermute | solution.py:14
  849.0 47.4 %collective-permute-start.10 = (f32[2,2,128,1024]{3,2,1,0:T(8,128)S(1)}, f32[2,2,128,1024]{3,2,1,0:T(8,128)S(1)}, u32[]{:S(2)}, u32[]{:S(2)}) collective-permute-start(f32[2,2,128,1024]{3,2,1,0:T(8,128)S(1)} %pad_maximum_fusion.9), channel_id=1, source_target_pairs={{0,16},{1,17},{2,18},{3,19},{4,20},{5,21},{6,22},{7,23},{8,24},{9,... | collective-permute-start | bytes 6291464 | tf_op jit(solution)/shard_map/ppermute | solution.py:14
  897.0 1.1 copy-start.10
  897.0 1.2 copy-start.14
  897.0 1.2 copy-start.17
  897.0 1.2 copy-start.18
  977.4 5.1 collective-permute-start.11
Sparse Core Ops, SparseCore 0:
  979.4 60.7 all-reduce.3
where the time goes:
time: 1050 us
  waiting for transfers between devices  860 us (82%)
  blocking collectives  76.6 us (7%)
  other arithmetic  50.7 us (5%)
  starting transfers between devices  23.2 us (2%)
  between operations  15.3 us (1%)
  matrix products  14.2 us (1%)
    ppermute x10, waiting for transfers between devices, swapped(): return lax.ppermute(value, axis, pairs)  801 us
    psum x1, blocking collectives, per_device(): short_sum, skip_sum = lax.psum((short_part, skip_part), ('dp', 'ctx'))  76.6 us
    psum x1, waiting for transfers between devices, per_device(): filter_sum = lax.psum(filter_part, 'dp')  56.2 us
  transfers between devices with their start and end apart: 13, of which 12 were waited for; matrix products, arithmetic and copies ran while one was open for 0% of the time, Pallas kernels for 0%

commit v1 on v0

v1 whole, which is shorter than its diff:
```python
import functools
import math

import jax
import jax.numpy as jnp
import ml_dtypes
import numpy as np
from jax import lax
from jax.experimental import pallas as pl
from jax.experimental.pallas import tpu as pltpu
from jax.sharding import PartitionSpec as P

MESH = pl.DeviceIdType.MESH
F32 = jnp.float32
BF16 = jnp.bfloat16

DP = 8
CTX = 32
TOK = 128
CH = 512
GRP = 16
TAPS = 7


def tables():
    index = np.arange(TOK)
    angle = 2.0 * np.pi * (np.outer(index, index) % TOK) / TOK
    cos, sin = np.cos(angle), np.sin(angle)
    forward = np.block([[cos, -sin], [sin, cos]])
    inverse = np.block([[cos, sin], [-sin, cos]]) / (CTX * TOK)
    parts = []
    for matrix in (forward, inverse):
        high = matrix.astype(np.float32).astype(ml_dtypes.bfloat16)
        low = (matrix - high.astype(np.float64)).astype(np.float32).astype(ml_dtypes.bfloat16)
        parts += [high, low]
    weights = np.stack(parts)
    inner = np.zeros((8, 8, TOK), np.float32)
    for a0 in range(8):
        for j0 in range(4):
            turn = -2.0 * np.pi * a0 * (1 + 4 * j0) / 128
            inner[a0, 2 * j0], inner[a0, 2 * j0 + 1] = np.cos(turn), np.sin(turn)
    outer = np.zeros((4, 16, TOK), np.float32)
    for j0 in range(4):
        for j1 in range(8):
            turn = -2.0 * np.pi * index * (4 * (j0 + 4 * j1) + 1) / 16384
            outer[j0, 2 * j1], outer[j0, 2 * j1 + 1] = np.cos(turn), np.sin(turn)
    return weights, inner, outer


COS1, SIN1 = math.cos(math.pi / 8), math.sin(math.pi / 8)
ROOT = math.sqrt(0.5)
COS3, SIN3 = math.cos(3 * math.pi / 8), math.sin(3 * math.pi / 8)


def cadd(x, y):
    return (x[0] + y[0], x[1] + y[1])


def csub(x, y):
    return (x[0] - y[0], x[1] - y[1])


def cmul(x, y):
    return (x[0] * y[0] - x[1] * y[1], x[0] * y[1] + x[1] * y[0])


def cmul_conj(x, y):
    return (x[0] * y[0] + x[1] * y[1], x[1] * y[0] - x[0] * y[1])


def turn(x, sign):
    return (-x[1], x[0]) if sign > 0 else (x[1], -x[0])


def dft4(x, sign):
    even, odd = cadd(x[0], x[2]), cadd(x[1], x[3])
    even1, odd1 = csub(x[0], x[2]), turn(csub(x[1], x[3]), sign)
    return [cadd(even, odd), cadd(even1, odd1), csub(even, odd), csub(even1, odd1)]


def dft8(x, sign):
    even = dft4(x[0::2], sign)
    odd = dft4(x[1::2], sign)
    first, third = odd[1], odd[3]
    if sign < 0:
        odd[1] = ((first[0] + first[1]) * ROOT, (first[1] - first[0]) * ROOT)
        odd[3] = ((third[1] - third[0]) * ROOT, (third[0] + third[1]) * -ROOT)
    else:
        odd[1] = ((first[0] - first[1]) * ROOT, (first[1] + first[0]) * ROOT)
        odd[3] = ((third[0] + third[1]) * -ROOT, (third[0] - third[1]) * ROOT)
    odd[2] = turn(odd[2], sign)
    return [cadd(even[k], odd[k]) for k in range(4)] + [csub(even[k], odd[k]) for k in range(4)]


def store_split(split_ref, slot, value):
    for half in range(2):
        high = value[half].astype(BF16)
        low = (value[half] - high.astype(F32)).astype(BF16)
        split_ref[slot, :, half * TOK : (half + 1) * TOK] = high
        split_ref[slot, :, (2 + half) * TOK : (3 + half) * TOK] = low


def product(split_ref, weights_ref, which, out_ref):
    rows = CTX * GRP
    high = split_ref[:, :, : 2 * TOK].reshape(rows, 2 * TOK)
    low = split_ref[:, :, 2 * TOK :].reshape(rows, 2 * TOK)
    dot = functools.partial(jnp.dot, preferred_element_type=F32)
    total = dot(high, weights_ref[which + 1]) + dot(low, weights_ref[which])
    total = total + dot(high, weights_ref[which])
    out_ref[...] = total.reshape(CTX, GRP, 2 * TOK)


def load_complex(ref, slot):
    return (ref[slot, :, :TOK], ref[slot, :, TOK:])


def transform(load, half_ref, split_ref, inner_ref, outer_ref, weights_ref, out_ref):
    def first(a0, carry):
        x0, x1, x2, x3 = [load(a0 + 8 * a1) for a1 in range(4)]
        t1 = (x1 * COS1, x1 * -SIN1)
        t2 = x2 * ROOT
        t3 = (x3 * COS3, x3 * -SIN3)
        even, even1 = (x0 + t2, -t2), (x0 - t2, t2)
        odd, odd1 = cadd(t1, t3), turn(csub(t1, t3), -1)
        for j0, value in enumerate([cadd(even, odd), cadd(even1, odd1), csub(even, odd), csub(even1, odd1)]):
            factor = (inner_ref[a0, 2 * j0 : 2 * j0 + 1, :], inner_ref[a0, 2 * j0 + 1 : 2 * j0 + 2, :])
            value = cmul(value, factor)
            half_ref[j0, a0, 0] = value[0]
            half_ref[j0, a0, 1] = value[1]
        return carry

    lax.fori_loop(0, 8, first, 0)

    def second(j0, carry):
        values = dft8([(half_ref[j0, a0, 0], half_ref[j0, a0, 1]) for a0 in range(8)], -1)
        for j1, value in enumerate(values):
            factor = (outer_ref[j0, 2 * j1 : 2 * j1 + 1, :], outer_ref[j0, 2 * j1 + 1 : 2 * j1 + 2, :])
            store_split(split_ref, j0 * 8 + j1, cmul(value, factor))
        return carry

    lax.fori_loop(0, 4, second, 0)
    product(split_ref, weights_ref, 0, out_ref)


def inverse(pair, emit, half_ref, split_ref, inner_ref, outer_ref, weights_ref, work_ref):
    def multiply(slot, carry):
        store_split(split_ref, slot, pair(slot))
        return carry

    lax.fori_loop(0, CTX, multiply, 0)
    product(split_ref, weights_ref, 2, work_ref)

    def second(j0, carry):
        values = []
        for j1 in range(8):
            factor = (outer_ref[j0, 2 * j1 : 2 * j1 + 1, :], outer_ref[j0, 2 * j1 + 1 : 2 * j1 + 2, :])
            values.append(cmul_conj(load_complex(work_ref, j0 * 8 + j1), factor))
        for a0, value in enumerate(dft8(values, 1)):
            half_ref[j0, a0, 0] = value[0]
            half_ref[j0, a0, 1] = value[1]
        return carry

    lax.fori_loop(0, 4, second, 0)

    def first(a0, carry):
        values = []
        for j0 in range(4):
            factor = (inner_ref[a0, 2 * j0 : 2 * j0 + 1, :], inner_ref[a0, 2 * j0 + 1 : 2 * j0 + 2, :])
            values.append(cmul_conj((half_ref[j0, a0, 0], half_ref[j0, a0, 1]), factor))
        z0, z1, z2, z3 = dft4(values, 1)
        emit(a0, z0[0])
        emit(a0 + 8, z1[0] * COS1 - z1[1] * SIN1)
        emit(a0 + 16, (z2[0] - z2[1]) * ROOT)
        emit(a0 + 24, z3[0] * COS3 - z3[1] * SIN3)
        return carry

    lax.fori_loop(0, 8, first, 0)


def kernel(
    feat_ref, cot_ref, filt_ref, short_ref, skip_ref, weights_ref, inner_ref, outer_ref,
    out_ref, gfeat_ref, gshort_ref, gfilt_ref, gskip_ref,
    send_in, recv_in, send_filt, part_filt, all_filt, send_out, recv_out, send_corr, recv_corr,
    mine_corr, part_grad, all_grad, tap_rows, tap_cols, taps, key_ref, value_ref, query_ref,
    gated_ref, dconv_ref, conv_ref, dgated_ref, half_ref, split_ref, spec_g, spec_h, spec_d, work_ref,
    sems_send, sems_recv, sem_local,
):
    dp, me = lax.axis_index("dp"), lax.axis_index("ctx")
    zed, row = lax.rem(me, 8), me // 8
    owner = zed == dp
    owner_count = jnp.where(owner, 1, 0)
    lane = lax.broadcasted_iota(jnp.int32, (GRP, TOK), 1)
    scale = 1.0 / math.sqrt(DP * CTX * TOK)

    barrier = pltpu.get_barrier_semaphore()

    def greet(dp_index, ctx_index):
        pl.semaphore_signal(barrier, inc=1, device_id={"dp": dp_index, "ctx": ctx_index}, device_id_type=MESH)

    def greet_ctx(step, carry):
        greet(dp, lax.rem(me + step, CTX))
        return carry

    lax.fori_loop(1, CTX, greet_ctx, 0)

    def greet_dp(step, carry):
        greet(lax.rem(dp + step, DP), me)
        return carry

    lax.fori_loop(1, DP, greet_dp, 0)
    for x in range(4):

        @pl.when(jnp.logical_not(jnp.logical_and(owner, row == x)))
        def _():
            greet(zed, 8 * x + dp)

    def pack(block, part, slot, base):
        columns = [base + TOK * k for k in range(4)]
        for k, start in enumerate(columns):
            tile = block[:, start : start + TOK].T
            send_in[part, 8 * k : 8 * k + 8, slot * GRP : (slot + 1) * GRP, :] = tile.reshape(8, GRP, TOK)

    for k in range(4):
        send_filt[8 * k : 8 * k + 8] = filt_ref[:, k * TOK : (k + 1) * TOK].T.reshape(8, GRP, TOK)
    pack(feat_ref, 0, 0, CH)
    pack(feat_ref, 0, 1, 2 * CH)
    pack(feat_ref, 1, 0, 0)
    pack(cot_ref, 1, 1, 0)

    pl.semaphore_wait(barrier, (CTX - 1) + (DP - 1) + 4 - owner_count)

    def remote(src, dst, index, dp_index, ctx_index):
        return pltpu.make_async_remote_copy(
            src_ref=src,
            dst_ref=dst,
            send_sem=sems_send.at[index],
            recv_sem=sems_recv.at[index],
            device_id={"dp": dp_index, "ctx": ctx_index},
            device_id_type=MESH,
        )

    def await_bytes(ref, sem):
        pltpu.make_async_copy(ref, ref, sem).wait()

    def to_ctx(make):
        def step_to(step, carry):
            make(lax.rem(me + step, CTX)).start()
            return carry

        lax.fori_loop(1, CTX, step_to, 0)

    def to_dp(make):
        def step_to(step, carry):
            make(lax.rem(dp + step, DP)).start()
            return carry

        lax.fori_loop(1, DP, step_to, 0)

    def cross(source, target_ref, index):
        for x in range(4):
            itself = jnp.logical_and(owner, row == x)

            @pl.when(jnp.logical_not(itself))
            def _():
                remote(source(x), target_ref.at[row], index, zed, 8 * x + dp).start()

            @pl.when(itself)
            def _():
                pltpu.make_async_copy(source(x), target_ref.at[row], sems_recv.at[index]).start()

    cross(lambda x: send_filt.at[8 * x + dp], part_filt, 0)
    to_ctx(lambda c: remote(send_in.at[0, c], recv_in.at[0, me], 2, dp, c))
    await_bytes(part_filt, sems_recv.at[0])
    to_dp(lambda d: remote(part_filt, all_filt.at[dp], 1, d, me))
    to_ctx(lambda c: remote(send_in.at[1, c], recv_in.at[1, me], 3, dp, c))
    all_filt[dp] = part_filt[...]
    recv_in[0, me] = send_in[0, me]
    recv_in[1, me] = send_in[1, me]

    for stream in range(3):
        for k in range(4):
            start = stream * CH + k * TOK
            tap_rows[k, 8 * stream : 8 * stream + TAPS, :] = short_ref[:, start : start + TOK]
            if stream == 0:
                tap_rows[k, TAPS : TAPS + 1, :] = skip_ref[:, k * TOK : (k + 1) * TOK]
            else:
                tap_rows[k, 8 * stream + TAPS : 8 * stream + 8, :] = jnp.zeros((1, TOK), F32)
    chosen = tap_rows[me // 8]
    tap_cols[...] = jnp.concatenate([chosen, jnp.zeros((TOK - 24, TOK), F32)], axis=0).T
    mine = tap_cols[pl.ds(pl.multiple_of(lax.rem(me, 8) * GRP, GRP), GRP), :]
    for index in range(24):
        taps[index] = jnp.broadcast_to(mine[:, index : index + 1], (GRP, TOK))

    common = (half_ref, split_ref, inner_ref, outer_ref, weights_ref)

    await_bytes(all_filt.at[pl.ds(0, DP - 1)], sems_recv.at[1])
    transform(lambda a: all_filt[lax.rem(a, 8), a // 8], *common, spec_h)

    def mix(source, before, first_tap):
        total = taps[first_tap] * source
        for tap in range(1, TAPS):
            moved = pltpu.roll(jnp.where(lane >= TOK - tap, before, source), tap, axis=1)
            total = total + taps[first_tap + tap] * moved
        return total

    await_bytes(recv_in.at[0, pl.ds(0, CTX - 1)], sems_recv.at[2])

    def mix_pair(a, carry):
        key = recv_in[0, a, :GRP, :].astype(F32)
        value = recv_in[0, a, GRP:, :].astype(F32)
        mixed_key = mix(key, carry[0], 8)
        mixed_value = mix(value, carry[1], 16)
        key_ref[a] = mixed_key
        value_ref[a] = mixed_value
        gated_ref[a] = mixed_key * mixed_value
        return (key, value)

    zero = jnp.zeros((GRP, TOK), F32)
    lax.fori_loop(0, CTX, mix_pair, (zero, zero))
    transform(lambda a: gated_ref[a], *common, spec_g)

    def emit_conv(a, value):
        conv_ref[a] = value + taps[TAPS] * gated_ref[a]

    inverse(lambda s: cmul(load_complex(spec_g, s), load_complex(spec_h, s)), emit_conv, *common, work_ref)

    await_bytes(recv_in.at[1, pl.ds(0, CTX - 1)], sems_recv.at[3])

    def mix_query(a, carry):
        query = recv_in[1, a, :GRP, :].astype(F32)
        mixed = mix(query, carry, 0)
        query_ref[a] = mixed
        dconv_ref[a] = mixed * recv_in[1, a, GRP:, :].astype(F32)
        return query

    lax.fori_loop(0, CTX, mix_query, zero)

    def back_mix(current, after, first_tap, source, sums):
        total = taps[first_tap] * current
        out_sums = [sums[0] + current * source]
        for tap in range(1, TAPS):
            moved = pltpu.roll(jnp.where(lane < tap, after, current), TOK - tap, axis=1)
            total = total + taps[first_tap + tap] * moved
            out_sums.append(sums[tap] + moved * source)
        return total, out_sums

    def back_query(step, carry):
        a = CTX - 1 - step
        after, skip_sum, sums = carry[0], carry[1], carry[2:]
        conv = conv_ref[a]
        send_out[0, a, :GRP, :] = (query_ref[a] * conv).astype(BF16)
        current = recv_in[1, a, GRP:, :].astype(F32) * conv
        total, sums = back_mix(current, after, 0, recv_in[1, a, :GRP, :].astype(F32), sums)
        send_out[0, a, GRP:, :] = total.astype(BF16)
        return (current, skip_sum + dconv_ref[a] * gated_ref[a], *sums)

    sums_query = lax.fori_loop(0, CTX, back_query, (zero,) * 9)[1:]
    to_ctx(lambda c: remote(send_out.at[0, c], recv_out.at[0, me], 4, dp, c))
    recv_out[0, me] = send_out[0, me]

    def collect(start, columns, small):
        for offset, column in enumerate(columns):
            small = jnp.where(lane == start + offset, jnp.sum(column, axis=1, keepdims=True), small)
        return small

    small = collect(TAPS, sums_query[:1], zero)
    small = collect(0, sums_query[1:], small)

    transform(lambda a: dconv_ref[a], *common, spec_d)

    def emit_back(a, value):
        dgated_ref[a] = value + taps[TAPS] * dconv_ref[a]

    inverse(lambda s: cmul_conj(load_complex(spec_d, s), load_complex(spec_h, s)), emit_back, *common, work_ref)

    for slot, (partner, first_tap) in enumerate([(value_ref, 8), (key_ref, 16)]):

        def back_pair(step, carry, slot=slot, partner=partner, first_tap=first_tap):
            a = CTX - 1 - step
            rows = slice(slot * GRP, (slot + 1) * GRP)
            current = dgated_ref[a] * partner[a]
            total, sums = back_mix(current, carry[0], first_tap, recv_in[0, a, rows, :].astype(F32), carry[1:])
            send_out[1, a, rows, :] = total.astype(BF16)
            return (current, *sums)

        small = collect(first_tap, lax.fori_loop(0, CTX, back_pair, (zero,) * 8)[1:], small)

    to_ctx(lambda c: remote(send_out.at[1, c], recv_out.at[1, me], 5, dp, c))
    recv_out[1, me] = send_out[1, me]

    def emit_corr(a, value):
        send_corr[lax.rem(a, 8), a // 8] = value * scale

    inverse(lambda s: cmul_conj(load_complex(spec_d, s), load_complex(spec_g, s)), emit_corr, *common, work_ref)
    for member in range(DP):
        send_corr[member, 4] = small * scale
    to_dp(lambda d: remote(send_corr.at[d], recv_corr.at[dp], 6, d, me))
    recv_corr[dp] = send_corr[dp]

    def unpack(part, slot, target_ref, base):
        for k in range(4):
            tile = recv_out[part, 8 * k : 8 * k + 8, slot * GRP : (slot + 1) * GRP, :].reshape(TOK, TOK)
            target_ref[:, base + k * TOK : base + (k + 1) * TOK] = tile.T

    await_bytes(recv_corr.at[pl.ds(0, DP - 1)], sems_recv.at[6])
    total = recv_corr[0]
    for member in range(1, DP):
        total = total + recv_corr[member]
    mine_corr[...] = total

    cross(lambda x: mine_corr.at[x], part_grad, 7)

    @pl.when(owner)
    def _():
        pltpu.make_async_copy(mine_corr.at[4], part_grad.at[4 + row], sems_recv.at[7]).start()
        to_ctx(lambda c: remote(mine_corr.at[4], part_grad.at[4 + row], 8, dp, c))

    @pl.when(owner)
    def _():
        await_bytes(part_grad.at[pl.ds(0, 5)], sems_recv.at[7])
        await_bytes(part_grad.at[pl.ds(0, 3)], sems_recv.at[8])

    @pl.when(jnp.logical_not(owner))
    def _():
        await_bytes(part_grad.at[pl.ds(0, 4)], sems_recv.at[7])
        await_bytes(part_grad.at[pl.ds(0, 4)], sems_recv.at[8])

    to_dp(lambda d: remote(part_grad, all_grad.at[dp], 9, d, me))
    all_grad[dp] = part_grad[...]

    await_bytes(recv_out.at[0, pl.ds(0, CTX - 1)], sems_recv.at[4])
    unpack(0, 0, out_ref, 0)
    unpack(0, 1, gfeat_ref, 0)
    await_bytes(recv_out.at[1, pl.ds(0, CTX - 1)], sems_recv.at[5])
    unpack(1, 0, gfeat_ref, CH)
    unpack(1, 1, gfeat_ref, 2 * CH)

    await_bytes(all_grad.at[pl.ds(0, DP - 1)], sems_recv.at[9])
    for x in range(4):
        columns = slice(x * TOK, (x + 1) * TOK)
        gfilt_ref[:, columns] = all_grad[:, x].reshape(TOK, TOK).T
        rows = all_grad[:, 4 + x].reshape(TOK, TOK).T
        gskip_ref[:, columns] = rows[TAPS : TAPS + 1, :]
        for stream in range(3):
            gshort_ref[:, stream * CH + x * TOK : stream * CH + (x + 1) * TOK] = rows[8 * stream : 8 * stream + TAPS, :]

    @pl.when(owner)
    def _():
        await_bytes(send_filt.at[pl.ds(0, 3)], sems_send.at[0])
        await_bytes(mine_corr.at[pl.ds(0, 3)], sems_send.at[7])
        await_bytes(send_filt.at[pl.ds(0, CTX - 1)], sems_send.at[8])

    @pl.when(jnp.logical_not(owner))
    def _():
        await_bytes(send_filt.at[pl.ds(0, 4)], sems_send.at[0])
        await_bytes(mine_corr.at[pl.ds(0, 4)], sems_send.at[7])

    await_bytes(all_filt.at[pl.ds(0, DP - 1)], sems_send.at[1])
    for part in range(2):
        await_bytes(send_in.at[part, pl.ds(0, CTX - 1)], sems_send.at[2 + part])
        await_bytes(send_out.at[part, pl.ds(0, CTX - 1)], sems_send.at[4 + part])
    await_bytes(send_corr.at[pl.ds(0, DP - 1)], sems_send.at[6])
    await_bytes(all_grad.at[pl.ds(0, DP - 1)], sems_send.at[9])


def per_device(features, short_weight, long_filter, skip_bias, cotangent):
    weights, inner, outer = tables()
    vmem = pl.BlockSpec(memory_space=pltpu.VMEM)
    block = (CTX, GRP, TOK)
    out, gfeat, gshort, gfilt, gskip = pl.pallas_call(
        kernel,
        out_shape=(
            jax.ShapeDtypeStruct((TOK, CH), BF16),
            jax.ShapeDtypeStruct((TOK, 3 * CH), BF16),
            jax.ShapeDtypeStruct((TAPS, 3 * CH), F32),
            jax.ShapeDtypeStruct((TOK, CH), F32),
            jax.ShapeDtypeStruct((1, CH), F32),
        ),
        in_specs=[vmem] * 8,
        out_specs=(vmem,) * 5,
        scratch_shapes=[
            pltpu.VMEM((2, CTX, 2 * GRP, TOK), BF16),
            pltpu.VMEM((2, CTX, 2 * GRP, TOK), BF16),
            pltpu.VMEM(block, F32),
            pltpu.VMEM((4, GRP, TOK), F32),
            pltpu.VMEM((DP, 4, GRP, TOK), F32),
            pltpu.VMEM((2, CTX, 2 * GRP, TOK), BF16),
            pltpu.VMEM((2, CTX, 2 * GRP, TOK), BF16),
            pltpu.VMEM((DP, 5, GRP, TOK), F32),
            pltpu.VMEM((DP, 5, GRP, TOK), F32),
            pltpu.VMEM((5, GRP, TOK), F32),
            pltpu.VMEM((8, GRP, TOK), F32),
            pltpu.VMEM((DP, 8, GRP, TOK), F32),
            pltpu.VMEM((4, 24, TOK), F32),
            pltpu.VMEM((TOK, TOK), F32),
            pltpu.VMEM((24, GRP, TOK), F32),
            pltpu.VMEM(block, F32),
            pltpu.VMEM(block, F32),
            pltpu.VMEM(block, F32),
            pltpu.VMEM(block, F32),
            pltpu.VMEM(block, F32),
            pltpu.VMEM(block, F32),
            pltpu.VMEM(block, F32),
            pltpu.VMEM((4, 8, 2, GRP, TOK), F32),
            pltpu.VMEM((CTX, GRP, 4 * TOK), BF16),
            pltpu.VMEM((CTX, GRP, 2 * TOK), F32),
            pltpu.VMEM((CTX, GRP, 2 * TOK), F32),
            pltpu.VMEM((CTX, GRP, 2 * TOK), F32),
            pltpu.VMEM((CTX, GRP, 2 * TOK), F32),
            pltpu.SemaphoreType.DMA((10,)),
            pltpu.SemaphoreType.DMA((10,)),
            pltpu.SemaphoreType.DMA,
        ],
        compiler_params=pltpu.CompilerParams(
            collective_id=0, has_side_effects=True, vmem_limit_bytes=40 << 20
        ),
        name="hyena",
    )(
        features[0], cotangent[0], long_filter, short_weight, skip_bias.reshape(1, CH),
        jnp.asarray(weights), jnp.asarray(inner), jnp.asarray(outer),
    )
    return (out[None], gfeat[None], gshort, gfilt, gskip.reshape(CH))


def solution(mesh):
    return jax.shard_map(
        per_device,
        mesh=mesh,
        in_specs=(P("dp", "ctx", None), P(), P("ctx", None), P(), P("dp", "ctx", None)),
        out_specs=(P("dp", "ctx", None), P("dp", "ctx", None), P(), P("ctx", None), P()),
        check_vma=False,
    )
```

time: 1050 us -> 77.9 us (0.07)
  waiting for transfers between devices: 860 us -> 0 us
  blocking collectives: 76.6 us -> 0 us
  Pallas kernels: 0 us -> 66.6 us
  other arithmetic: 50.7 us -> 0 us
  starting transfers between devices: 23.2 us -> 0 us
  between operations: 15.3 us -> 0.66 us
  matrix products: 14.2 us -> 0 us
    ppermute x12 -> x0, waiting for transfers between devices: 804 us -> none  [the longest x10 801 us: swapped(): return lax.ppermute(value, axis, pairs)]
    psum x1 -> x0, blocking collectives: 76.6 us -> none  [per_device(): short_sum, skip_sum = lax.psum((short_part, skip_part), ('dp', 'ctx'))]
    pallas_call x0 -> x1, Pallas kernels: none -> 66.6 us  [per_device(): pl.pallas_call(kernel, out_shape=(jax.ShapeDtypeStruct((TOK, CH), BF16),...]
    psum x1 -> x0, waiting for transfers between devices: 56.2 us -> none  [per_device(): filter_sum = lax.psum(filter_part, 'dp')]
    ppermute x12 -> x0, starting transfers between devices: 23.2 us -> none  [the longest x10 17.5 us: swapped(): return lax.ppermute(value, axis, pairs)]
    another operation x13 -> x0, other arithmetic: 15.6 us -> none  [the longest x6 10.5 us: butterfly_forward(): partner = pair_swap(jnp.stack([spec_real, spec_imag]), bit_place)]
    add x8 -> x0, other arithmetic: 14.3 us -> none  [the longest x3 7.03 us: butterfly_inverse(): turned_imag = spec_imag * cos_turn + spec_real * sin_turn]
    dot_general x8 -> x0, matrix products: 14.2 us -> none  [the longest x4 7.91 us: contract(): return jnp.einsum('akm,amw->akw', matrix, values, precision=PRECISE)]
  transfers between devices with their start and end apart: 13 -> 0, of which waited for: 12 -> 0; matrix products, arithmetic and copies ran while one was open for 0% -> 0% of each run, Pallas kernels for 0% -> 0%
where the time goes in v1:
time: 77.9 us; the launch traced here: 77.5 us
  Pallas kernels  66.6 us (85%)
  local copies, waits for them, and re-layouts  10.2 us (13%)
    pallas_call x1, Pallas kernels, per_device(): pl.pallas_call(kernel, out_shape=(jax.ShapeDtypeStruct((TOK, CH), BF16),...  66.6 us
    unnamed x21, local copies, waits for them, and re-layouts  10.2 us

profile of v1, /device:TPU:1, one launch (start us, length us, event | category | flops | bytes accessed | tf_op | source)
XLA Modules:
  0.0 77.5 jit_solution(8104969541257632722)
XLA Ops:
  0.6 0.0 copy-start.7
  0.6 0.7 copy-done.7
  1.3 0.0 copy-start
  1.3 1.0 %copy-done = bf16[4,256,256]{2,1,0:T(8,128)(2,1)S(1)} copy-done((bf16[4,256,256]{2,1,0:T(8,128)(2,1)S(1)}, bf16[4,256,256]{2,1,0:T(8,128)(2,1)}, u32[]{:S(2)}) %copy-start) | copy-done | bytes 524312
  2.4 0.0 copy-start.1
  2.4 1.0 %copy-done.1 = bf16[1,128,1536]{2,1,0:T(8,128)(2,1)S(1)} copy-done((bf16[1,128,1536]{2,1,0:T(8,128)(2,1)S(1)}, bf16[1,128,1536]{2,1,0:T(8,128)(2,1)}, u32[]{:S(2)}) %copy-start.1) | copy-done | bytes 393240
  3.4 0.0 copy-start.2
  3.4 0.9 %copy-done.2 = f32[128,512]{1,0:T(8,128)S(1)} copy-done((f32[128,512]{1,0:T(8,128)S(1)}, f32[128,512]{1,0:T(8,128)}, u32[]{:S(2)}) %copy-start.2) | copy-done | bytes 262168
  4.3 0.0 copy-start.3
  4.3 0.9 %copy-done.3 = bf16[1,128,512]{2,1,0:T(8,128)(2,1)S(1)} copy-done((bf16[1,128,512]{2,1,0:T(8,128)(2,1)S(1)}, bf16[1,128,512]{2,1,0:T(8,128)(2,1)}, u32[]{:S(2)}) %copy-start.3) | copy-done | bytes 131096
  5.2 0.0 copy-start.4
  5.2 0.8 %copy-done.4 = f32[7,1536]{1,0:T(8,128)S(1)} copy-done((f32[7,1536]{1,0:T(8,128)S(1)}, f32[7,1536]{1,0:T(8,128)}, u32[]{:S(2)}) %copy-start.4) | copy-done | bytes 43032
  6.0 0.0 copy-start.5
  6.0 0.8 copy-done.5
  6.8 0.0 copy-start.6
  6.8 0.8 copy-done.6
  7.5 66.6 %hyena.1 = (bf16[128,512]{1,0:T(8,128)(2,1)S(1)}, bf16[128,1536]{1,0:T(8,128)(2,1)S(1)}, f32[7,1536]{1,0:T(8,128)S(1)}, f32[128,512]{1,0:T(8,128)S(1)}, f32[1,512]{1,0:T(1,128)S(1)}) custom-call(bf16[128,1536]{1,0:T(8,128)(2,1)S(1)} %bitcast.7, bf16[128,512]{1,0:T(8,128)(2,1)S(1)} %bitcast.9, f32[128,512]{1,0:T(8,128)S(1)} %copy-done.2, ...), custom_call_target="tpu_custom_call" | custom-call | tf_op jit(solution)/shard_map/hyena/pallas_call | solution.py:470
  74.1 0.7 copy.18
  74.8 0.7 copy.19
  75.6 0.6 copy.20
  76.2 0.7 copy.21
  76.9 0.6 copy.22
Async XLA Ops:
  0.6 0.7 copy-start.7
  1.3 1.0 %copy-start = (bf16[4,256,256]{2,1,0:T(8,128)(2,1)S(1)}, bf16[4,256,256]{2,1,0:T(8,128)(2,1)}, u32[]{:S(2)}) copy-start(bf16[4,256,256]{2,1,0:T(8,128)(2,1)} %constant.6.clone.weights_ref) | copy-start | bytes 1572868
  2.4 1.0 %copy-start.1 = (bf16[1,128,1536]{2,1,0:T(8,128)(2,1)S(1)}, bf16[1,128,1536]{2,1,0:T(8,128)(2,1)}, u32[]{:S(2)}) copy-start(bf16[1,128,1536]{2,1,0:T(8,128)(2,1)} %param.8) | copy-start | bytes 1179652
  3.4 0.9 %copy-start.2 = (f32[128,512]{1,0:T(8,128)S(1)}, f32[128,512]{1,0:T(8,128)}, u32[]{:S(2)}) copy-start(f32[128,512]{1,0:T(8,128)} %filt_ref.1) | copy-start | bytes 786436
  4.3 0.9 %copy-start.3 = (bf16[1,128,512]{2,1,0:T(8,128)(2,1)S(1)}, bf16[1,128,512]{2,1,0:T(8,128)(2,1)}, u32[]{:S(2)}) copy-start(bf16[1,128,512]{2,1,0:T(8,128)(2,1)} %param.12) | copy-start | bytes 393220
  5.2 0.8 %copy-start.4 = (f32[7,1536]{1,0:T(8,128)S(1)}, f32[7,1536]{1,0:T(8,128)}, u32[]{:S(2)}) copy-start(f32[7,1536]{1,0:T(8,128)} %short_ref.1) | copy-start | bytes 129028
  6.0 0.8 copy-start.5
  6.8 0.8 copy-start.6

commit v2 on v1

--- a/solution.py
+++ b/solution.py
@@ -178,13 +178,25 @@
 
 
 def kernel(
+    feat_hbm, cot_hbm, filt_hbm, short_hbm, skip_hbm, weights_hbm, inner_hbm, outer_hbm,
+    out_ref, gfeat_ref, gshort_ref, gfilt_ref, gskip_ref,
     feat_ref, cot_ref, filt_ref, short_ref, skip_ref, weights_ref, inner_ref, outer_ref,
-    out_ref, gfeat_ref, gshort_ref, gfilt_ref, gskip_ref,
     send_in, recv_in, send_filt, part_filt, all_filt, send_out, recv_out, send_corr, recv_corr,
     mine_corr, part_grad, all_grad, tap_rows, tap_cols, taps, key_ref, value_ref, query_ref,
     gated_ref, dconv_ref, conv_ref, dgated_ref, half_ref, split_ref, spec_g, spec_h, spec_d, work_ref,
-    sems_send, sems_recv, sem_local,
+    small_send, small_dp, small_zed, small_row, sems_send, sems_recv, sems_load,
 ):
+    loads = [
+        pltpu.make_async_copy(source, target, sems_load.at[index])
+        for index, (source, target) in enumerate(
+            [
+                (filt_hbm, filt_ref), (feat_hbm, feat_ref), (cot_hbm, cot_ref), (short_hbm, short_ref),
+                (skip_hbm, skip_ref), (inner_hbm, inner_ref), (outer_hbm, outer_ref), (weights_hbm, weights_ref),
+            ]
+        )
+    ]
+    for load in loads:
+        load.start()
     dp, me = lax.axis_index("dp"), lax.axis_index("ctx")
     zed, row = lax.rem(me, 8), me // 8
     owner = zed == dp
@@ -220,11 +232,14 @@
             tile = block[:, start : start + TOK].T
             send_in[part, 8 * k : 8 * k + 8, slot * GRP : (slot + 1) * GRP, :] = tile.reshape(8, GRP, TOK)
 
+    loads[0].wait()
     for k in range(4):
         send_filt[8 * k : 8 * k + 8] = filt_ref[:, k * TOK : (k + 1) * TOK].T.reshape(8, GRP, TOK)
+    loads[1].wait()
     pack(feat_ref, 0, 0, CH)
     pack(feat_ref, 0, 1, 2 * CH)
     pack(feat_ref, 1, 0, 0)
+    loads[2].wait()
     pack(cot_ref, 1, 1, 0)
 
     pl.semaphore_wait(barrier, (CTX - 1) + (DP - 1) + 4 - owner_count)
@@ -276,6 +291,9 @@
     all_filt[dp] = part_filt[...]
     recv_in[0, me] = send_in[0, me]
     recv_in[1, me] = send_in[1, me]
+
+    for load in loads[3:]:
+        load.wait()
 
     for stream in range(3):
         for k in range(4):
@@ -316,7 +334,7 @@
         return (key, value)
 
     zero = jnp.zeros((GRP, TOK), F32)
-    lax.fori_loop(0, CTX, mix_pair, (zero, zero))
+    lax.fori_loop(0, CTX, mix_pair, (zero, zero), unroll=4)
     transform(lambda a: gated_ref[a], *common, spec_g)
 
     def emit_conv(a, value):
@@ -333,7 +351,7 @@
         dconv_ref[a] = mixed * recv_in[1, a, GRP:, :].astype(F32)
         return query
 
-    lax.fori_loop(0, CTX, mix_query, zero)
+    lax.fori_loop(0, CTX, mix_query, zero, unroll=4)
 
     def back_mix(current, after, first_tap, source, sums):
         total = taps[first_tap] * current
@@ -354,7 +372,7 @@
         send_out[0, a, GRP:, :] = total.astype(BF16)
         return (current, skip_sum + dconv_ref[a] * gated_ref[a], *sums)
 
-    sums_query = lax.fori_loop(0, CTX, back_query, (zero,) * 9)[1:]
+    sums_query = lax.fori_loop(0, CTX, back_query, (zero,) * 9, unroll=4)[1:]
     to_ctx(lambda c: remote(send_out.at[0, c], recv_out.at[0, me], 4, dp, c))
     recv_out[0, me] = send_out[0, me]
 
@@ -372,6 +390,13 @@
         dgated_ref[a] = value + taps[TAPS] * dconv_ref[a]
 
     inverse(lambda s: cmul_conj(load_complex(spec_d, s), load_complex(spec_h, s)), emit_back, *common, work_ref)
+
+    def emit_corr(a, value):
+        send_corr[lax.rem(a, 8), a // 8] = value * scale
+
+    inverse(lambda s: cmul_conj(load_complex(spec_d, s), load_complex(spec_g, s)), emit_corr, *common, work_ref)
+    to_dp(lambda d: remote(send_corr.at[d], recv_corr.at[dp], 6, d, me))
+    recv_corr[dp] = send_corr[dp]
 
     for slot, (partner, first_tap) in enumerate([(value_ref, 8), (key_ref, 16)]):
 
@@ -383,72 +408,67 @@
             send_out[1, a, rows, :] = total.astype(BF16)
             return (current, *sums)
 
-        small = collect(first_tap, lax.fori_loop(0, CTX, back_pair, (zero,) * 8)[1:], small)
-
+        small = collect(first_tap, lax.fori_loop(0, CTX, back_pair, (zero,) * 8, unroll=4)[1:], small)
+
+    tap_cols[...] = jnp.zeros((TOK, TOK), F32)
+    tap_cols[pl.ds(pl.multiple_of(zed * GRP, GRP), GRP), :] = small * scale
+    small_send[0] = tap_cols[...].T[:24, :]
+    small_dp[dp] = small_send[0]
+    to_dp(lambda d: remote(small_send.at[0], small_dp.at[dp], 8, d, me))
     to_ctx(lambda c: remote(send_out.at[1, c], recv_out.at[1, me], 5, dp, c))
     recv_out[1, me] = send_out[1, me]
-
-    def emit_corr(a, value):
-        send_corr[lax.rem(a, 8), a // 8] = value * scale
-
-    inverse(lambda s: cmul_conj(load_complex(spec_d, s), load_complex(spec_g, s)), emit_corr, *common, work_ref)
-    for member in range(DP):
-        send_corr[member, 4] = small * scale
-    to_dp(lambda d: remote(send_corr.at[d], recv_corr.at[dp], 6, d, me))
-    recv_corr[dp] = send_corr[dp]
 
     def unpack(part, slot, target_ref, base):
         for k in range(4):
             tile = recv_out[part, 8 * k : 8 * k + 8, slot * GRP : (slot + 1) * GRP, :].reshape(TOK, TOK)
             target_ref[:, base + k * TOK : base + (k + 1) * TOK] = tile.T
 
+    def summed(ref):
+        total = ref[0]
+        for index in range(1, 8):
+            total = total + ref[index]
+        return total
+
     await_bytes(recv_corr.at[pl.ds(0, DP - 1)], sems_recv.at[6])
-    total = recv_corr[0]
-    for member in range(1, DP):
-        total = total + recv_corr[member]
-    mine_corr[...] = total
-
+    mine_corr[...] = summed(recv_corr)
     cross(lambda x: mine_corr.at[x], part_grad, 7)
 
-    @pl.when(owner)
-    def _():
-        pltpu.make_async_copy(mine_corr.at[4], part_grad.at[4 + row], sems_recv.at[7]).start()
-        to_ctx(lambda c: remote(mine_corr.at[4], part_grad.at[4 + row], 8, dp, c))
-
-    @pl.when(owner)
-    def _():
-        await_bytes(part_grad.at[pl.ds(0, 5)], sems_recv.at[7])
-        await_bytes(part_grad.at[pl.ds(0, 3)], sems_recv.at[8])
-
-    @pl.when(jnp.logical_not(owner))
-    def _():
-        await_bytes(part_grad.at[pl.ds(0, 4)], sems_recv.at[7])
-        await_bytes(part_grad.at[pl.ds(0, 4)], sems_recv.at[8])
-
+    await_bytes(small_dp.at[pl.ds(0, DP - 1)], sems_recv.at[8])
+    small_send[1] = summed(small_dp)
+    small_zed[zed] = small_send[1]
+    for step in range(1, 8):
+        remote(small_send.at[1], small_zed.at[zed], 10, dp, 8 * row + lax.rem(zed + step, 8)).start()
+
+    await_bytes(part_grad, sems_recv.at[7])
     to_dp(lambda d: remote(part_grad, all_grad.at[dp], 9, d, me))
     all_grad[dp] = part_grad[...]
+
+    await_bytes(small_zed.at[pl.ds(0, 7)], sems_recv.at[10])
+    small_send[2] = summed(small_zed)
+    small_row[row] = small_send[2]
+    for step in range(1, 4):
+        remote(small_send.at[2], small_row.at[row], 11, dp, 8 * lax.rem(row + step, 4) + zed).start()
 
     await_bytes(recv_out.at[0, pl.ds(0, CTX - 1)], sems_recv.at[4])
     unpack(0, 0, out_ref, 0)
     unpack(0, 1, gfeat_ref, 0)
+    await_bytes(small_row.at[pl.ds(0, 3)], sems_recv.at[11])
+    for x in range(4):
+        gskip_ref[:, x * TOK : (x + 1) * TOK] = small_row[x, TAPS : TAPS + 1, :]
+        for stream in range(3):
+            columns = slice(stream * CH + x * TOK, stream * CH + (x + 1) * TOK)
+            gshort_ref[:, columns] = small_row[x, 8 * stream : 8 * stream + TAPS, :]
     await_bytes(recv_out.at[1, pl.ds(0, CTX - 1)], sems_recv.at[5])
     unpack(1, 0, gfeat_ref, CH)
     unpack(1, 1, gfeat_ref, 2 * CH)
-
     await_bytes(all_grad.at[pl.ds(0, DP - 1)], sems_recv.at[9])
     for x in range(4):
-        columns = slice(x * TOK, (x + 1) * TOK)
-        gfilt_ref[:, columns] = all_grad[:, x].reshape(TOK, TOK).T
-        rows = all_grad[:, 4 + x].reshape(TOK, TOK).T
-        gskip_ref[:, columns] = rows[TAPS : TAPS + 1, :]
-        for stream in range(3):
-            gshort_ref[:, stream * CH + x * TOK : stream * CH + (x + 1) * TOK] = rows[8 * stream : 8 * stream + TAPS, :]
+        gfilt_ref[:, x * TOK : (x + 1) * TOK] = all_grad[:, x].reshape(TOK, TOK).T
 
     @pl.when(owner)
     def _():
         await_bytes(send_filt.at[pl.ds(0, 3)], sems_send.at[0])
         await_bytes(mine_corr.at[pl.ds(0, 3)], sems_send.at[7])
-        await_bytes(send_filt.at[pl.ds(0, CTX - 1)], sems_send.at[8])
 
     @pl.when(jnp.logical_not(owner))
     def _():
@@ -460,25 +480,52 @@
         await_bytes(send_in.at[part, pl.ds(0, CTX - 1)], sems_send.at[2 + part])
         await_bytes(send_out.at[part, pl.ds(0, CTX - 1)], sems_send.at[4 + part])
     await_bytes(send_corr.at[pl.ds(0, DP - 1)], sems_send.at[6])
+    await_bytes(small_dp.at[pl.ds(0, DP - 1)], sems_send.at[8])
     await_bytes(all_grad.at[pl.ds(0, DP - 1)], sems_send.at[9])
+    await_bytes(small_zed.at[pl.ds(0, 7)], sems_send.at[10])
+    await_bytes(small_row.at[pl.ds(0, 3)], sems_send.at[11])
+
+
+def deliver(*refs):
+    sources, targets, sems = refs[:5], refs[5:10], refs[10]
+    copies = [pltpu.make_async_copy(sources[index], targets[index], sems.at[index]) for index in range(5)]
+    for copy in copies:
+        copy.start()
+    for copy in copies:
+        copy.wait()
 
 
 def per_device(features, short_weight, long_filter, skip_bias, cotangent):
     weights, inner, outer = tables()
+    hbm = pl.BlockSpec(memory_space=pltpu.HBM)
     vmem = pl.BlockSpec(memory_space=pltpu.VMEM)
     block = (CTX, GRP, TOK)
-    out, gfeat, gshort, gfilt, gskip = pl.pallas_call(
+    shapes = (
+        jax.ShapeDtypeStruct((TOK, CH), BF16),
+        jax.ShapeDtypeStruct((TOK, 3 * CH), BF16),
+        jax.ShapeDtypeStruct((TAPS, 3 * CH), F32),
+        jax.ShapeDtypeStruct((TOK, CH), F32),
+        jax.ShapeDtypeStruct((1, CH), F32),
+    )
+    operands = [
+        features[0], cotangent[0], long_filter, short_weight, skip_bias.reshape(1, CH),
+        jnp.asarray(weights), jnp.asarray(inner), jnp.asarray(outer),
+    ]
+    operands = [pltpu.with_memory_space_constraint(operand, pltpu.HBM) for operand in operands]
+    results = pl.pallas_call(
         kernel,
-        out_shape=(
-            jax.ShapeDtypeStruct((TOK, CH), BF16),
-            jax.ShapeDtypeStruct((TOK, 3 * CH), BF16),
-            jax.ShapeDtypeStruct((TAPS, 3 * CH), F32),
-            jax.ShapeDtypeStruct((TOK, CH), F32),
-            jax.ShapeDtypeStruct((1, CH), F32),
-        ),
-        in_specs=[vmem] * 8,
+        out_shape=shapes,
+        in_specs=[hbm] * 8,
         out_specs=(vmem,) * 5,
         scratch_shapes=[
+            pltpu.VMEM((TOK, 3 * CH), BF16),
+            pltpu.VMEM((TOK, CH), BF16),
+            pltpu.VMEM((TOK, CH), F32),
+            pltpu.VMEM((TAPS, 3 * CH), F32),
+            pltpu.VMEM((1, CH), F32),
+            pltpu.VMEM(weights.shape, BF16),
+            pltpu.VMEM(inner.shape, F32),
+            pltpu.VMEM(outer.shape, F32),
             pltpu.VMEM((2, CTX, 2 * GRP, TOK), BF16),
             pltpu.VMEM((2, CTX, 2 * GRP, TOK), BF16),
             pltpu.VMEM(block, F32),
@@ -486,11 +533,11 @@
             pltpu.VMEM((DP, 4, GRP, TOK), F32),
             pltpu.VMEM((2, CTX, 2 * GRP, TOK), BF16),
             pltpu.VMEM((2, CTX, 2 * GRP, TOK), BF16),
-            pltpu.VMEM((DP, 5, GRP, TOK), F32),
-            pltpu.VMEM((DP, 5, GRP, TOK), F32),
-            pltpu.VMEM((5, GRP, TOK), F32),
-            pltpu.VMEM((8, GRP, TOK), F32),
-            pltpu.VMEM((DP, 8, GRP, TOK), F32),
+            pltpu.VMEM((DP, 4, GRP, TOK), F32),
+            pltpu.VMEM((DP, 4, GRP, TOK), F32),
+            pltpu.VMEM((4, GRP, TOK), F32),
+            pltpu.VMEM((4, GRP, TOK), F32),
+            pltpu.VMEM((DP, 4, GRP, TOK), F32),
             pltpu.VMEM((4, 24, TOK), F32),
             pltpu.VMEM((TOK, TOK), F32),
             pltpu.VMEM((24, GRP, TOK), F32),
@@ -507,18 +554,28 @@
             pltpu.VMEM((CTX, GRP, 2 * TOK), F32),
             pltpu.VMEM((CTX, GRP, 2 * TOK), F32),
             pltpu.VMEM((CTX, GRP, 2 * TOK), F32),
-            pltpu.SemaphoreType.DMA((10,)),
-            pltpu.SemaphoreType.DMA((10,)),
-            pltpu.SemaphoreType.DMA,
+            pltpu.VMEM((3, 24, TOK), F32),
+            pltpu.VMEM((DP, 24, TOK), F32),
+            pltpu.VMEM((8, 24, TOK), F32),
+            pltpu.VMEM((4, 24, TOK), F32),
+            pltpu.SemaphoreType.DMA((12,)),
+            pltpu.SemaphoreType.DMA((12,)),
+            pltpu.SemaphoreType.DMA((8,)),
         ],
         compiler_params=pltpu.CompilerParams(
             collective_id=0, has_side_effects=True, vmem_limit_bytes=40 << 20
         ),
         name="hyena",
-    )(
-        features[0], cotangent[0], long_filter, short_weight, skip_bias.reshape(1, CH),
-        jnp.asarray(weights), jnp.asarray(inner), jnp.asarray(outer),
-    )
+    )(*operands)
+    out, gfeat, gshort, gfilt, gskip = pl.pallas_call(
+        deliver,
+        out_shape=shapes,
+        in_specs=[vmem] * 5,
+        out_specs=(hbm,) * 5,
+        scratch_shapes=[pltpu.SemaphoreType.DMA((5,))],
+        compiler_params=pltpu.CompilerParams(vmem_limit_bytes=4 << 20),
+        name="deliver",
+    )(*results)
     return (out[None], gfeat[None], gshort, gfilt, gskip.reshape(CH))
 
 

time: 77.9 us -> 55.1 us (0.71)
  Pallas kernels: 66.6 us -> 54.4 us
  local copies, waits for them, and re-layouts: 10.2 us -> 0 us
    pallas_call x1 -> x2, Pallas kernels: 66.6 us -> 54.4 us  [the longest x1 53.5 us: per_device(): pl.pallas_call(kernel, out_shape=shapes, in_specs=[hbm] * 8, out_specs=(v...]
    unnamed x21 -> x0, local copies, waits for them, and re-layouts: 10.2 us -> none
where the time goes in v2:
time: 55.1 us; the launch traced here: 55 us
  Pallas kernels  54.4 us (99%)
  between operations  0.64 us (1%)
    pallas_call x1, Pallas kernels, per_device(): pl.pallas_call(kernel, out_shape=shapes, in_specs=[hbm] * 8, out_specs=(v...  53.5 us

profile of v2, /device:TPU:1, one launch (start us, length us, event | category | flops | bytes accessed | tf_op | source)
XLA Modules:
  0.0 55.0 jit_solution(4109858048386102519)
XLA Ops:
  0.6 53.5 %hyena.1 = (bf16[128,512]{1,0:T(8,128)(2,1)S(1)}, bf16[128,1536]{1,0:T(8,128)(2,1)S(1)}, f32[7,1536]{1,0:T(8,128)S(1)}, f32[128,512]{1,0:T(8,128)S(1)}, f32[1,512]{1,0:T(1,128)S(1)}) custom-call(bf16[128,1536]{1,0:T(8,128)(2,1)} %bitcast.6, bf16[128,512]{1,0:T(8,128)(2,1)} %bitcast.7, f32[128,512]{1,0:T(8,128)} %filt_hbm.1, f32[7,1536]{1,0:T(8,128)} %short_hbm.1, ...), custom_call_target="tpu_custom_call" | custom-call | tf_op jit(solution)/shard_map/hyena/pallas_call | solution.py:515
  54.1 0.9 %deliver.1 = (bf16[128,512]{1,0:T(8,128)(2,1)}, bf16[128,1536]{1,0:T(8,128)(2,1)}, f32[7,1536]{1,0:T(8,128)}, f32[128,512]{1,0:T(8,128)}, f32[1,512]{1,0:T(1,128)}) custom-call(bf16[128,512]{1,0:T(8,128)(2,1)S(1)} %get-tuple-element.15.refs_0_, bf16[128,1536]{1,0:T(8,128)(2,1)S(1)} %get-tuple-element.16.refs_1_, f32[7,1536]{1,0:T(8,128)S(1)} %get-tuple-element.17.refs_2_, ...), custom_call_target="tpu_custom_call" | custom-call | tf_op jit(solution)/shard_map/deliver/pallas_call | solution.py:570

commit v3 on v2

--- a/solution.py
+++ b/solution.py
@@ -101,13 +101,14 @@
 
 
 def product(split_ref, weights_ref, which, out_ref):
-    rows = CTX * GRP
-    high = split_ref[:, :, : 2 * TOK].reshape(rows, 2 * TOK)
-    low = split_ref[:, :, 2 * TOK :].reshape(rows, 2 * TOK)
     dot = functools.partial(jnp.dot, preferred_element_type=F32)
-    total = dot(high, weights_ref[which + 1]) + dot(low, weights_ref[which])
-    total = total + dot(high, weights_ref[which])
-    out_ref[...] = total.reshape(CTX, GRP, 2 * TOK)
+    for start in range(0, CTX, 8):
+        rows = slice(start, start + 8)
+        high = split_ref[rows, :, : 2 * TOK].reshape(TOK, 2 * TOK)
+        low = split_ref[rows, :, 2 * TOK :].reshape(TOK, 2 * TOK)
+        total = dot(high, weights_ref[which + 1]) + dot(low, weights_ref[which])
+        total = total + dot(high, weights_ref[which])
+        out_ref[rows] = total.reshape(8, GRP, 2 * TOK)
 
 
 def load_complex(ref, slot):
@@ -129,7 +130,7 @@
             half_ref[j0, a0, 1] = value[1]
         return carry
 
-    lax.fori_loop(0, 8, first, 0)
+    lax.fori_loop(0, 8, first, 0, unroll=2)
 
     def second(j0, carry):
         values = dft8([(half_ref[j0, a0, 0], half_ref[j0, a0, 1]) for a0 in range(8)], -1)
@@ -147,7 +148,7 @@
         store_split(split_ref, slot, pair(slot))
         return carry
 
-    lax.fori_loop(0, CTX, multiply, 0)
+    lax.fori_loop(0, CTX, multiply, 0, unroll=4)
     product(split_ref, weights_ref, 2, work_ref)
 
     def second(j0, carry):
@@ -174,7 +175,7 @@
         emit(a0 + 24, z3[0] * COS3 - z3[1] * SIN3)
         return carry
 
-    lax.fori_loop(0, 8, first, 0)
+    lax.fori_loop(0, 8, first, 0, unroll=2)
 
 
 def kernel(
@@ -184,7 +185,7 @@
     send_in, recv_in, send_filt, part_filt, all_filt, send_out, recv_out, send_corr, recv_corr,
     mine_corr, part_grad, all_grad, tap_rows, tap_cols, taps, key_ref, value_ref, query_ref,
     gated_ref, dconv_ref, conv_ref, dgated_ref, half_ref, split_ref, spec_g, spec_h, spec_d, work_ref,
-    small_send, small_dp, small_zed, small_row, sems_send, sems_recv, sems_load,
+    small_send, small_dp, small_ctx, sems_send, sems_recv, sems_load,
 ):
     loads = [
         pltpu.make_async_copy(source, target, sems_load.at[index])
@@ -285,9 +286,9 @@
 
     cross(lambda x: send_filt.at[8 * x + dp], part_filt, 0)
     to_ctx(lambda c: remote(send_in.at[0, c], recv_in.at[0, me], 2, dp, c))
+    to_ctx(lambda c: remote(send_in.at[1, c], recv_in.at[1, me], 3, dp, c))
     await_bytes(part_filt, sems_recv.at[0])
     to_dp(lambda d: remote(part_filt, all_filt.at[dp], 1, d, me))
-    to_ctx(lambda c: remote(send_in.at[1, c], recv_in.at[1, me], 3, dp, c))
     all_filt[dp] = part_filt[...]
     recv_in[0, me] = send_in[0, me]
     recv_in[1, me] = send_in[1, me]
@@ -353,6 +354,15 @@
 
     lax.fori_loop(0, CTX, mix_query, zero, unroll=4)
 
+    transform(lambda a: dconv_ref[a], *common, spec_d)
+
+    def emit_corr(a, value):
+        send_corr[lax.rem(a, 8), a // 8] = value * scale
+
+    inverse(lambda s: cmul_conj(load_complex(spec_d, s), load_complex(spec_g, s)), emit_corr, *common, work_ref)
+    to_dp(lambda d: remote(send_corr.at[d], recv_corr.at[dp], 6, d, me))
+    recv_corr[dp] = send_corr[dp]
+
     def back_mix(current, after, first_tap, source, sums):
         total = taps[first_tap] * current
         out_sums = [sums[0] + current * source]
@@ -384,19 +394,10 @@
     small = collect(TAPS, sums_query[:1], zero)
     small = collect(0, sums_query[1:], small)
 
-    transform(lambda a: dconv_ref[a], *common, spec_d)
-
     def emit_back(a, value):
         dgated_ref[a] = value + taps[TAPS] * dconv_ref[a]
 
     inverse(lambda s: cmul_conj(load_complex(spec_d, s), load_complex(spec_h, s)), emit_back, *common, work_ref)
-
-    def emit_corr(a, value):
-        send_corr[lax.rem(a, 8), a // 8] = value * scale
-
-    inverse(lambda s: cmul_conj(load_complex(spec_d, s), load_complex(spec_g, s)), emit_corr, *common, work_ref)
-    to_dp(lambda d: remote(send_corr.at[d], recv_corr.at[dp], 6, d, me))
-    recv_corr[dp] = send_corr[dp]
 
     for slot, (partner, first_tap) in enumerate([(value_ref, 8), (key_ref, 16)]):
 
@@ -410,19 +411,6 @@
 
         small = collect(first_tap, lax.fori_loop(0, CTX, back_pair, (zero,) * 8, unroll=4)[1:], small)
 
-    tap_cols[...] = jnp.zeros((TOK, TOK), F32)
-    tap_cols[pl.ds(pl.multiple_of(zed * GRP, GRP), GRP), :] = small * scale
-    small_send[0] = tap_cols[...].T[:24, :]
-    small_dp[dp] = small_send[0]
-    to_dp(lambda d: remote(small_send.at[0], small_dp.at[dp], 8, d, me))
-    to_ctx(lambda c: remote(send_out.at[1, c], recv_out.at[1, me], 5, dp, c))
-    recv_out[1, me] = send_out[1, me]
-
-    def unpack(part, slot, target_ref, base):
-        for k in range(4):
-            tile = recv_out[part, 8 * k : 8 * k + 8, slot * GRP : (slot + 1) * GRP, :].reshape(TOK, TOK)
-            target_ref[:, base + k * TOK : base + (k + 1) * TOK] = tile.T
-
     def summed(ref):
         total = ref[0]
         for index in range(1, 8):
@@ -433,37 +421,55 @@
     mine_corr[...] = summed(recv_corr)
     cross(lambda x: mine_corr.at[x], part_grad, 7)
 
+    tap_cols[...] = jnp.zeros((TOK, TOK), F32)
+    tap_cols[pl.ds(pl.multiple_of(zed * GRP, GRP), GRP), :] = small * scale
+    turned = tap_cols[...].T
+    tile = turned[:8, :]
+    for stream in (1, 2):
+        tile = tile + pltpu.roll(turned[8 * stream : 8 * stream + 8, :], GRP * stream, axis=1)
+    small_send[0] = tile
+    small_dp[dp] = tile
+    to_dp(lambda d: remote(small_send.at[0], small_dp.at[dp], 8, d, me))
+    to_ctx(lambda c: remote(send_out.at[1, c], recv_out.at[1, me], 5, dp, c))
+    recv_out[1, me] = send_out[1, me]
+
+    def unpack(part, slot, target_ref, base):
+        for k in range(4):
+            tile = recv_out[part, 8 * k : 8 * k + 8, slot * GRP : (slot + 1) * GRP, :].reshape(TOK, TOK)
+            target_ref[:, base + k * TOK : base + (k + 1) * TOK] = tile.T
+
     await_bytes(small_dp.at[pl.ds(0, DP - 1)], sems_recv.at[8])
     small_send[1] = summed(small_dp)
-    small_zed[zed] = small_send[1]
-    for step in range(1, 8):
-        remote(small_send.at[1], small_zed.at[zed], 10, dp, 8 * row + lax.rem(zed + step, 8)).start()
+    small_ctx[me] = small_send[1]
+    to_ctx(lambda c: remote(small_send.at[1], small_ctx.at[me], 10, dp, c))
 
     await_bytes(part_grad, sems_recv.at[7])
     to_dp(lambda d: remote(part_grad, all_grad.at[dp], 9, d, me))
     all_grad[dp] = part_grad[...]
 
-    await_bytes(small_zed.at[pl.ds(0, 7)], sems_recv.at[10])
-    small_send[2] = summed(small_zed)
-    small_row[row] = small_send[2]
-    for step in range(1, 4):
-        remote(small_send.at[2], small_row.at[row], 11, dp, 8 * lax.rem(row + step, 4) + zed).start()
-
     await_bytes(recv_out.at[0, pl.ds(0, CTX - 1)], sems_recv.at[4])
     unpack(0, 0, out_ref, 0)
     unpack(0, 1, gfeat_ref, 0)
-    await_bytes(small_row.at[pl.ds(0, 3)], sems_recv.at[11])
-    for x in range(4):
-        gskip_ref[:, x * TOK : (x + 1) * TOK] = small_row[x, TAPS : TAPS + 1, :]
-        for stream in range(3):
-            columns = slice(stream * CH + x * TOK, stream * CH + (x + 1) * TOK)
-            gshort_ref[:, columns] = small_row[x, 8 * stream : 8 * stream + TAPS, :]
     await_bytes(recv_out.at[1, pl.ds(0, CTX - 1)], sems_recv.at[5])
     unpack(1, 0, gfeat_ref, CH)
     unpack(1, 1, gfeat_ref, 2 * CH)
     await_bytes(all_grad.at[pl.ds(0, DP - 1)], sems_recv.at[9])
     for x in range(4):
         gfilt_ref[:, x * TOK : (x + 1) * TOK] = all_grad[:, x].reshape(TOK, TOK).T
+
+    await_bytes(small_ctx.at[pl.ds(0, CTX - 1)], sems_recv.at[10])
+    place = lax.broadcasted_iota(jnp.int32, (8, TOK), 1) // GRP
+    for x in range(4):
+        for stream in range(3):
+            rows = small_ctx[8 * x]
+            for z in range(1, 8):
+                rows = jnp.where(place == (z + stream) % 8, small_ctx[8 * x + z], rows)
+            if stream:
+                rows = pltpu.roll(rows, TOK - GRP * stream, axis=1)
+            columns = slice(stream * CH + x * TOK, stream * CH + (x + 1) * TOK)
+            gshort_ref[:, columns] = rows[:TAPS, :]
+            if stream == 0:
+                gskip_ref[:, columns] = rows[TAPS:, :]
 
     @pl.when(owner)
     def _():
@@ -482,8 +488,7 @@
     await_bytes(send_corr.at[pl.ds(0, DP - 1)], sems_send.at[6])
     await_bytes(small_dp.at[pl.ds(0, DP - 1)], sems_send.at[8])
     await_bytes(all_grad.at[pl.ds(0, DP - 1)], sems_send.at[9])
-    await_bytes(small_zed.at[pl.ds(0, 7)], sems_send.at[10])
-    await_bytes(small_row.at[pl.ds(0, 3)], sems_send.at[11])
+    await_bytes(small_ctx.at[pl.ds(0, CTX - 1)], sems_send.at[10])
 
 
 def deliver(*refs):
@@ -554,10 +559,9 @@
             pltpu.VMEM((CTX, GRP, 2 * TOK), F32),
             pltpu.VMEM((CTX, GRP, 2 * TOK), F32),
             pltpu.VMEM((CTX, GRP, 2 * TOK), F32),
-            pltpu.VMEM((3, 24, TOK), F32),
-            pltpu.VMEM((DP, 24, TOK), F32),
-            pltpu.VMEM((8, 24, TOK), F32),
-            pltpu.VMEM((4, 24, TOK), F32),
+            pltpu.VMEM((2, 8, TOK), F32),
+            pltpu.VMEM((DP, 8, TOK), F32),
+            pltpu.VMEM((CTX, 8, TOK), F32),
             pltpu.SemaphoreType.DMA((12,)),
             pltpu.SemaphoreType.DMA((12,)),
             pltpu.SemaphoreType.DMA((8,)),

time: 55.1 us -> 52.3 us (0.949)
  Pallas kernels: 54.4 us -> 51.2 us
    pallas_call x1, Pallas kernels: 53.5 us -> 50.3 us  [per_device(): pl.pallas_call(kernel, out_shape=shapes, in_specs=[hbm] * 8, out_specs=(v...]
where the time goes in v3:
time: 52.3 us; the launch traced here: 51.9 us
  Pallas kernels  51.2 us (98%)
  between operations  0.64 us (1%)
    pallas_call x1, Pallas kernels, per_device(): pl.pallas_call(kernel, out_shape=shapes, in_specs=[hbm] * 8, out_specs=(v...  50.3 us

profile of v3, /device:TPU:1, one launch (start us, length us, event | category | flops | bytes accessed | tf_op | source)
XLA Modules:
  0.0 51.9 jit_solution(189931099022617533)
XLA Ops:
  0.6 50.3 %hyena.1 = (bf16[128,512]{1,0:T(8,128)(2,1)S(1)}, bf16[128,1536]{1,0:T(8,128)(2,1)S(1)}, f32[7,1536]{1,0:T(8,128)S(1)}, f32[128,512]{1,0:T(8,128)S(1)}, f32[1,512]{1,0:T(1,128)S(1)}) custom-call(bf16[128,1536]{1,0:T(8,128)(2,1)} %bitcast.6, bf16[128,512]{1,0:T(8,128)(2,1)} %bitcast.7, f32[128,512]{1,0:T(8,128)} %filt_hbm.1, f32[7,1536]{1,0:T(8,128)} %short_hbm.1, ...), custom_call_target="tpu_custom_call" | custom-call | tf_op jit(solution)/shard_map/hyena/pallas_call | solution.py:520
  50.9 0.9 %deliver.1 = (bf16[128,512]{1,0:T(8,128)(2,1)}, bf16[128,1536]{1,0:T(8,128)(2,1)}, f32[7,1536]{1,0:T(8,128)}, f32[128,512]{1,0:T(8,128)}, f32[1,512]{1,0:T(1,128)}) custom-call(bf16[128,512]{1,0:T(8,128)(2,1)S(1)} %get-tuple-element.15.refs_0_, bf16[128,1536]{1,0:T(8,128)(2,1)S(1)} %get-tuple-element.16.refs_1_, f32[7,1536]{1,0:T(8,128)S(1)} %get-tuple-element.17.refs_2_, ...), custom_call_target="tpu_custom_call" | custom-call | tf_op jit(solution)/shard_map/deliver/pallas_call | solution.py:574

commit v4 on v3

--- a/solution.py
+++ b/solution.py
@@ -187,6 +187,35 @@
     gated_ref, dconv_ref, conv_ref, dgated_ref, half_ref, split_ref, spec_g, spec_h, spec_d, work_ref,
     small_send, small_dp, small_ctx, sems_send, sems_recv, sems_load,
 ):
+    dp, me = lax.axis_index("dp"), lax.axis_index("ctx")
+    zed, row = lax.rem(me, 8), me // 8
+    owner = zed == dp
+    owner_count = jnp.where(owner, 1, 0)
+    lane = lax.broadcasted_iota(jnp.int32, (GRP, TOK), 1)
+    scale = 1.0 / math.sqrt(DP * CTX * TOK)
+
+    barrier = pltpu.get_barrier_semaphore()
+
+    def greet(dp_index, ctx_index):
+        pl.semaphore_signal(barrier, inc=1, device_id={"dp": dp_index, "ctx": ctx_index}, device_id_type=MESH)
+
+    def greet_ctx(step, carry):
+        greet(dp, lax.rem(me + step, CTX))
+        return carry
+
+    lax.fori_loop(1, CTX, greet_ctx, 0)
+
+    def greet_dp(step, carry):
+        greet(lax.rem(dp + step, DP), me)
+        return carry
+
+    lax.fori_loop(1, DP, greet_dp, 0)
+    for x in range(4):
+
+        @pl.when(jnp.logical_not(jnp.logical_and(owner, row == x)))
+        def _():
+            greet(zed, 8 * x + dp)
+
     loads = [
         pltpu.make_async_copy(source, target, sems_load.at[index])
         for index, (source, target) in enumerate(
@@ -198,35 +227,6 @@
     ]
     for load in loads:
         load.start()
-    dp, me = lax.axis_index("dp"), lax.axis_index("ctx")
-    zed, row = lax.rem(me, 8), me // 8
-    owner = zed == dp
-    owner_count = jnp.where(owner, 1, 0)
-    lane = lax.broadcasted_iota(jnp.int32, (GRP, TOK), 1)
-    scale = 1.0 / math.sqrt(DP * CTX * TOK)
-
-    barrier = pltpu.get_barrier_semaphore()
-
-    def greet(dp_index, ctx_index):
-        pl.semaphore_signal(barrier, inc=1, device_id={"dp": dp_index, "ctx": ctx_index}, device_id_type=MESH)
-
-    def greet_ctx(step, carry):
-        greet(dp, lax.rem(me + step, CTX))
-        return carry
-
-    lax.fori_loop(1, CTX, greet_ctx, 0)
-
-    def greet_dp(step, carry):
-        greet(lax.rem(dp + step, DP), me)
-        return carry
-
-    lax.fori_loop(1, DP, greet_dp, 0)
-    for x in range(4):
-
-        @pl.when(jnp.logical_not(jnp.logical_and(owner, row == x)))
-        def _():
-            greet(zed, 8 * x + dp)
-
     def pack(block, part, slot, base):
         columns = [base + TOK * k for k in range(4)]
         for k, start in enumerate(columns):
@@ -352,7 +352,7 @@
         dconv_ref[a] = mixed * recv_in[1, a, GRP:, :].astype(F32)
         return query
 
-    lax.fori_loop(0, CTX, mix_query, zero, unroll=4)
+    lax.fori_loop(0, CTX, mix_query, zero, unroll=8)
 
     transform(lambda a: dconv_ref[a], *common, spec_d)
 
@@ -382,7 +382,7 @@
         send_out[0, a, GRP:, :] = total.astype(BF16)
         return (current, skip_sum + dconv_ref[a] * gated_ref[a], *sums)
 
-    sums_query = lax.fori_loop(0, CTX, back_query, (zero,) * 9, unroll=4)[1:]
+    sums_query = lax.fori_loop(0, CTX, back_query, (zero,) * 9, unroll=8)[1:]
     to_ctx(lambda c: remote(send_out.at[0, c], recv_out.at[0, me], 4, dp, c))
     recv_out[0, me] = send_out[0, me]
 
@@ -399,6 +399,7 @@
 
     inverse(lambda s: cmul_conj(load_complex(spec_d, s), load_complex(spec_h, s)), emit_back, *common, work_ref)
 
+    sums_pair = []
     for slot, (partner, first_tap) in enumerate([(value_ref, 8), (key_ref, 16)]):
 
         def back_pair(step, carry, slot=slot, partner=partner, first_tap=first_tap):
@@ -409,7 +410,7 @@
             send_out[1, a, rows, :] = total.astype(BF16)
             return (current, *sums)
 
-        small = collect(first_tap, lax.fori_loop(0, CTX, back_pair, (zero,) * 8, unroll=4)[1:], small)
+        sums_pair.append(lax.fori_loop(0, CTX, back_pair, (zero,) * 8, unroll=8)[1:])
 
     def summed(ref):
         total = ref[0]
@@ -421,6 +422,10 @@
     mine_corr[...] = summed(recv_corr)
     cross(lambda x: mine_corr.at[x], part_grad, 7)
 
+    to_ctx(lambda c: remote(send_out.at[1, c], recv_out.at[1, me], 5, dp, c))
+
+    for first_tap, sums in zip((8, 16), sums_pair):
+        small = collect(first_tap, sums, small)
     tap_cols[...] = jnp.zeros((TOK, TOK), F32)
     tap_cols[pl.ds(pl.multiple_of(zed * GRP, GRP), GRP), :] = small * scale
     turned = tap_cols[...].T
@@ -430,7 +435,6 @@
     small_send[0] = tile
     small_dp[dp] = tile
     to_dp(lambda d: remote(small_send.at[0], small_dp.at[dp], 8, d, me))
-    to_ctx(lambda c: remote(send_out.at[1, c], recv_out.at[1, me], 5, dp, c))
     recv_out[1, me] = send_out[1, me]
 
     def unpack(part, slot, target_ref, base):
@@ -450,12 +454,12 @@
     await_bytes(recv_out.at[0, pl.ds(0, CTX - 1)], sems_recv.at[4])
     unpack(0, 0, out_ref, 0)
     unpack(0, 1, gfeat_ref, 0)
+    await_bytes(all_grad.at[pl.ds(0, DP - 1)], sems_recv.at[9])
+    for x in range(4):
+        gfilt_ref[:, x * TOK : (x + 1) * TOK] = all_grad[:, x].reshape(TOK, TOK).T
     await_bytes(recv_out.at[1, pl.ds(0, CTX - 1)], sems_recv.at[5])
     unpack(1, 0, gfeat_ref, CH)
     unpack(1, 1, gfeat_ref, 2 * CH)
-    await_bytes(all_grad.at[pl.ds(0, DP - 1)], sems_recv.at[9])
-    for x in range(4):
-        gfilt_ref[:, x * TOK : (x + 1) * TOK] = all_grad[:, x].reshape(TOK, TOK).T
 
     await_bytes(small_ctx.at[pl.ds(0, CTX - 1)], sems_recv.at[10])
     place = lax.broadcasted_iota(jnp.int32, (8, TOK), 1) // GRP

time: 52.3 us -> 51.8 us (level)
    pallas_call x1, Pallas kernels: 50.3 us -> 49.8 us  [per_device(): pl.pallas_call(kernel, out_shape=shapes, in_specs=[hbm] * 8, out_specs=(v...]
where the time goes in v4:
time: 51.8 us; the launch traced here: 51.3 us
  Pallas kernels  50.7 us (98%)
  between operations  0.64 us (1%)
    pallas_call x1, Pallas kernels, per_device(): pl.pallas_call(kernel, out_shape=shapes, in_specs=[hbm] * 8, out_specs=(v...  49.8 us

profile of v4, /device:TPU:1, one launch (start us, length us, event | category | flops | bytes accessed | tf_op | source)
XLA Modules:
  0.0 51.3 jit_solution(8772366933772071722)
XLA Ops:
  0.6 49.8 %hyena.1 = (bf16[128,512]{1,0:T(8,128)(2,1)S(1)}, bf16[128,1536]{1,0:T(8,128)(2,1)S(1)}, f32[7,1536]{1,0:T(8,128)S(1)}, f32[128,512]{1,0:T(8,128)S(1)}, f32[1,512]{1,0:T(1,128)S(1)}) custom-call(bf16[128,1536]{1,0:T(8,128)(2,1)} %bitcast.6, bf16[128,512]{1,0:T(8,128)(2,1)} %bitcast.7, f32[128,512]{1,0:T(8,128)} %filt_hbm.1, f32[7,1536]{1,0:T(8,128)} %short_hbm.1, ...), custom_call_target="tpu_custom_call" | custom-call | tf_op jit(solution)/shard_map/hyena/pallas_call | solution.py:524
  50.4 0.9 %deliver.1 = (bf16[128,512]{1,0:T(8,128)(2,1)}, bf16[128,1536]{1,0:T(8,128)(2,1)}, f32[7,1536]{1,0:T(8,128)}, f32[128,512]{1,0:T(8,128)}, f32[1,512]{1,0:T(1,128)}) custom-call(bf16[128,512]{1,0:T(8,128)(2,1)S(1)} %get-tuple-element.15.refs_0_, bf16[128,1536]{1,0:T(8,128)(2,1)S(1)} %get-tuple-element.16.refs_1_, f32[7,1536]{1,0:T(8,128)S(1)} %get-tuple-element.17.refs_2_, ...), custom_call_target="tpu_custom_call" | custom-call | tf_op jit(solution)/shard_map/deliver/pallas_call | solution.py:578

commit v5 on v4

--- a/solution.py
+++ b/solution.py
@@ -130,7 +130,7 @@
             half_ref[j0, a0, 1] = value[1]
         return carry
 
-    lax.fori_loop(0, 8, first, 0, unroll=2)
+    lax.fori_loop(0, 8, first, 0, unroll=4)
 
     def second(j0, carry):
         values = dft8([(half_ref[j0, a0, 0], half_ref[j0, a0, 1]) for a0 in range(8)], -1)
@@ -139,7 +139,7 @@
             store_split(split_ref, j0 * 8 + j1, cmul(value, factor))
         return carry
 
-    lax.fori_loop(0, 4, second, 0)
+    lax.fori_loop(0, 4, second, 0, unroll=2)
     product(split_ref, weights_ref, 0, out_ref)
 
 
@@ -148,7 +148,7 @@
         store_split(split_ref, slot, pair(slot))
         return carry
 
-    lax.fori_loop(0, CTX, multiply, 0, unroll=4)
+    lax.fori_loop(0, CTX, multiply, 0, unroll=8)
     product(split_ref, weights_ref, 2, work_ref)
 
     def second(j0, carry):
@@ -161,7 +161,7 @@
             half_ref[j0, a0, 1] = value[1]
         return carry
 
-    lax.fori_loop(0, 4, second, 0)
+    lax.fori_loop(0, 4, second, 0, unroll=2)
 
     def first(a0, carry):
         values = []
@@ -175,7 +175,7 @@
         emit(a0 + 24, z3[0] * COS3 - z3[1] * SIN3)
         return carry
 
-    lax.fori_loop(0, 8, first, 0, unroll=2)
+    lax.fori_loop(0, 8, first, 0, unroll=4)
 
 
 def kernel(

time: 51.8 us -> 51.5 us (level)
  no operation moved by 1% of the time
where the time goes in v5:
time: 51.5 us; the launch traced here: 51.3 us
  Pallas kernels  50.7 us (98%)
  between operations  0.64 us (1%)
    pallas_call x1, Pallas kernels, per_device(): pl.pallas_call(kernel, out_shape=shapes, in_specs=[hbm] * 8, out_specs=(v...  49.7 us

profile of v5, /device:TPU:1, one launch (start us, length us, event | category | flops | bytes accessed | tf_op | source)
XLA Modules:
  0.0 51.3 jit_solution(9719186562402790802)
XLA Ops:
  0.6 49.7 %hyena.1 = (bf16[128,512]{1,0:T(8,128)(2,1)S(1)}, bf16[128,1536]{1,0:T(8,128)(2,1)S(1)}, f32[7,1536]{1,0:T(8,128)S(1)}, f32[128,512]{1,0:T(8,128)S(1)}, f32[1,512]{1,0:T(1,128)S(1)}) custom-call(bf16[128,1536]{1,0:T(8,128)(2,1)} %bitcast.6, bf16[128,512]{1,0:T(8,128)(2,1)} %bitcast.7, f32[128,512]{1,0:T(8,128)} %filt_hbm.1, f32[7,1536]{1,0:T(8,128)} %short_hbm.1, ...), custom_call_target="tpu_custom_call" | custom-call | tf_op jit(solution)/shard_map/hyena/pallas_call | solution.py:524
  50.4 0.9 %deliver.1 = (bf16[128,512]{1,0:T(8,128)(2,1)}, bf16[128,1536]{1,0:T(8,128)(2,1)}, f32[7,1536]{1,0:T(8,128)}, f32[128,512]{1,0:T(8,128)}, f32[1,512]{1,0:T(1,128)}) custom-call(bf16[128,512]{1,0:T(8,128)(2,1)S(1)} %get-tuple-element.15.refs_0_, bf16[128,1536]{1,0:T(8,128)(2,1)S(1)} %get-tuple-element.16.refs_1_, f32[7,1536]{1,0:T(8,128)S(1)} %get-tuple-element.17.refs_2_, ...), custom_call_target="tpu_custom_call" | custom-call | tf_op jit(solution)/shard_map/deliver/pallas_call | solution.py:578
